TPU v7x, 32 devices: a whole 2x2x4 slice. The times are simulated.
32 devices in a mesh: src: 16 (over z, y, core), tgt: 2 (over x).
Axes of the slice: x: 2, y: 2, z: 4, core: 2. Of those that a mesh axis runs over, the one named last changes fastest.
Arguments:
- src_emb: bfloat16 [8192, 1024], P('src', 'tgt'), may hold values from -16 to 16
- tgt_emb: bfloat16 [8192, 1024], P('tgt', 'src'), may hold values from -16 to 16
- src_ids: int32 [8192], P('src'), may hold values from 0 to 4095
- tgt_ids: int32 [8192], P('tgt'), may hold values from 0 to 4095
Outputs:
- margin: float32 [8192, 8192], P('src', 'tgt')
All inputs are finite; a program needn't handle non-finite values.
Results may differ from a plain program's by a relative error of at most 0.004.
Values may be sent and summed in bfloat16 or wider, within the bound.
A program may use at most 64 MiB of HBM per device.

v0:
```python
import functools

import jax
import jax.numpy as jnp
from jax import lax
from jax.experimental import pallas as pl
from jax.experimental.pallas import tpu as pltpu
from jax.sharding import PartitionSpec as P

epsilon = 1e-06
excluded_score = -2.0
MESH = pl.DeviceIdType.MESH
CHUNK = 512
EVERY = 8
OVER_AHEAD = 4
LAG = 1


def insert(best, value):
    out = []
    for level in best[:-1]:
        out.append(jnp.maximum(level, value))
        value = jnp.minimum(level, value)
    out.append(jnp.maximum(best[-1], value))
    return tuple(out)


def merge(first, second):
    c = [jnp.maximum(first[k], second[3 - k]) for k in range(4)]
    a, b = jnp.maximum(c[0], c[2]), jnp.maximum(c[1], c[3])
    d, e = jnp.minimum(c[0], c[2]), jnp.minimum(c[1], c[3])
    return (jnp.maximum(a, b), jnp.minimum(a, b), jnp.maximum(d, e), jnp.minimum(d, e))


def fold_sublanes(best):
    for shift in (4, 2, 1):
        best = merge(best, tuple(pltpu.roll(level, shift, 0) for level in best))
    return best


def stacked(best):
    row = lax.broadcasted_iota(jnp.int32, best[0].shape, 0)
    low = jnp.full(best[0].shape, -jnp.inf, jnp.float32)
    for k in range(3, -1, -1):
        low = jnp.where(row == k, best[k], low)
    return low


def lowest(shape):
    return tuple(jnp.full(shape, -jnp.inf, jnp.float32) for _ in range(4))


def kernel(dims, x_ref, a_ref, sid_ref, tid_ref, s_out, kt_out, ks_out, sids, g, a_whole, a_unit, b_unit, sbuf, rowbest,
           colbuf, colin, ktown, ktin, rowbuf, rowin, zrecv, zsend, yrecv, ysend, crecv, csend, arecv, asend, rrecv,
           rsend, krecv, ksend, mrecv, msend, lsem, osem):
    ns, nt, nz, chunks, cw, feats = dims
    s = lax.axis_index("src")
    t = lax.axis_index("tgt")
    z, y, c = s // 4, (s // 2) % 2, s % 2
    right = (s + 4, t)
    left = (s - 4, t)
    over = (z * 4 + (1 - y) * 2 + c, t)
    core = (s + 1 - 2 * c, t)
    rows = a_unit.shape[0]
    part = a_ref.shape[1]
    ow = colbuf.shape[2]
    has_right, has_left = z + 1 < nz, z >= 1

    def remote(src, dst, send, recv, where):
        return pltpu.make_async_remote_copy(
            src_ref=src, dst_ref=dst, send_sem=send, recv_sem=recv, device_id=where, device_id_type=MESH
        )

    def chunk_cols(j):
        return pl.ds(pl.multiple_of(j * cw, cw), cw)

    local = [
        pltpu.make_async_copy(x_ref.at[:, j * cw : (j + 1) * cw], g.at[j, z, y, c], lsem.at[1 + j]) for j in range(chunks)
    ]
    for copy in local:
        copy.start()
    acols = pl.ds(pl.multiple_of(t * part, part), part)
    local_a = pltpu.make_async_copy(a_ref, a_whole.at[:, acols], lsem.at[0])
    local_a.start()

    barrier = pltpu.get_barrier_semaphore()

    @pl.when(has_right)
    def _():
        pl.semaphore_signal(barrier, inc=1, device_id=right, device_id_type=MESH)

    @pl.when(has_left)
    def _():
        pl.semaphore_signal(barrier, inc=1, device_id=left, device_id_type=MESH)

    pl.semaphore_signal(barrier, inc=1, device_id=over, device_id_type=MESH)
    pl.semaphore_signal(barrier, inc=1, device_id=core, device_id_type=MESH)
    for k in range(1, nt):
        pl.semaphore_signal(barrier, inc=1, device_id=(s, lax.rem(t + k, nt)), device_id_type=MESH)
    pl.semaphore_wait(barrier, 1 + nt + has_right.astype(jnp.int32) + has_left.astype(jnp.int32))

    def y_first(j):
        return lax.rem(j, EVERY) == EVERY - 1

    def to_right(j, zp, yy):
        ref = g.at[j, zp, yy, c]
        return remote(ref, ref, zsend.at[0, j, zp, yy], zrecv.at[j, zp, yy], right)

    def to_left(j, zp, yy):
        ref = g.at[j, zp, yy, c]
        return remote(ref, ref, zsend.at[1, j, zp, yy], zrecv.at[j, zp, yy], left)

    def to_over(j, zp):
        ref = g.at[j, zp, y, c]
        return remote(ref, ref, ysend.at[j, zp], yrecv.at[j, zp], over)

    def from_over(j, zp):
        ref = g.at[j, zp, 1 - y, c]
        return remote(ref, ref, ysend.at[j, zp], yrecv.at[j, zp], over)

    def to_core(j, yy):
        ref = g.at[j, :, yy, c]
        return remote(ref, ref, csend.at[j, yy], crecv.at[j, yy], core)

    def from_core(j, yy):
        ref = g.at[j, :, yy, 1 - c]
        return remote(ref, ref, csend.at[j, yy], crecv.at[j, yy], core)

    def start_z(j, yy):
        @pl.when(has_right)
        def _():
            to_right(j, z, yy).start()

        @pl.when(has_left)
        def _():
            to_left(j, z, yy).start()

    def to_tgt(k):
        return remote(a_ref, a_whole.at[:, acols], asend.at[k], arecv.at[t], (s, lax.rem(t + k, nt)))

    ahead = min(2, chunks)
    behind = nz - 1 + LAG
    for copy in local:
        copy.wait()
    for j in range(ahead):
        start_z(j, y)
    for j in range(chunks):
        if j < OVER_AHEAD or j % EVERY == EVERY - 1:
            to_over(j, z).start()
    for k in range(1, nt):
        to_tgt(k).start()
    sids[...] = jnp.broadcast_to(sid_ref[...], (128, rows)).T

    def normalize_sources():
        local_a.wait()
        for k in range(1, nt):
            other = lax.rem(t + k, nt)
            cols = pl.ds(pl.multiple_of(other * part, part), part)
            remote(a_ref, a_whole.at[:, cols], asend.at[k], arecv.at[other], (s, other)).wait_recv()
        block = 16

        def step(r, carry):
            at = pl.ds(pl.multiple_of(r * block, block), block)
            v = a_whole[at, :].astype(jnp.float32)
            scale = jnp.sqrt(jnp.sum(v * v, axis=1, keepdims=True) + epsilon)
            a_unit[at, :] = (v / scale).astype(jnp.bfloat16)
            return carry

        lax.fori_loop(0, rows // block, step, 0)
        for k in range(4):
            rowbest[k] = jnp.full(rowbest.shape[1:], -jnp.inf, jnp.float32)

    def out_copy(j):
        return pltpu.make_async_copy(sbuf.at[j % 2], s_out.at[:, chunk_cols(j)], osem.at[j % 2])

    def compute(j):
        def squares(k, acc):
            v = g[j, k // 4, (k // 2) % 2, k % 2].astype(jnp.float32)
            return acc + jnp.sum((v * v).reshape(feats // 8, 8, cw), axis=0)

        acc = lax.fori_loop(0, ns, squares, jnp.zeros((8, cw), jnp.float32))
        inverse = 1.0 / jnp.sqrt(jnp.sum(acc, axis=0, keepdims=True) + epsilon)

        def scale(k, carry):
            v = g[j, k // 4, (k // 2) % 2, k % 2].astype(jnp.float32)
            b_unit[pl.ds(pl.multiple_of(k * feats, feats), feats), :] = (v * inverse).astype(jnp.bfloat16)
            return carry

        lax.fori_loop(0, ns, scale, 0)

        @pl.when(j >= 2)
        def _():
            out_copy(j - 2).wait()

        slot = j % 2
        sbuf[slot] = jnp.dot(a_unit[...], b_unit[...], preferred_element_type=jnp.float32)
        tids = jnp.broadcast_to(tid_ref[:, chunk_cols(j)], (8, cw))

        def group(r, best):
            at = pl.ds(pl.multiple_of(r * 8, 8), 8)
            ids = sids[at, :]
            row = tuple(rowbest[k, at, :] for k in range(4))
            pieces = []
            for q in range(cw // 128):
                lanes = pl.ds(q * 128, 128)
                v = sbuf[slot, at, lanes]
                v = jnp.where(ids == tids[:, q * 128 : (q + 1) * 128], jnp.float32(excluded_score), v)
                row = insert(row, v)
                sbuf[slot, at, lanes] = v
                pieces.append(v)
            for k in range(4):
                rowbest[k, at, :] = row[k]
            return tuple(insert(best[q], pieces[q]) for q in range(cw // 128))

        best = lax.fori_loop(0, rows // 8, group, tuple(lowest((8, 128)) for _ in range(cw // 128)), unroll=2)
        out_copy(j).start()
        per = ow // 128
        for q in range(cw // 128):
            colbuf[j * (cw // ow) + q // per, :, (q % per) * 128 : (q % per + 1) * 128] = stacked(fold_sublanes(best[q]))

    def within(j):
        return jnp.logical_and(j >= 0, j < chunks)

    def stage(j, d, first):
        both = (y, 1 - y) if first else (y,)

        @pl.when(z - d >= 0)
        def _():
            for yy in both:
                to_right(j, z - d, yy).wait_recv()

                @pl.when(has_right)
                def _():
                    to_right(j, z - d, yy).start()

            if not first:
                to_over(j, z - d).start()

        @pl.when(z + d < nz)
        def _():
            for yy in both:
                to_left(j, z + d, yy).wait_recv()

                @pl.when(has_left)
                def _():
                    to_left(j, z + d, yy).start()

            if not first:
                to_over(j, z + d).start()

        if d == nz - 1:
            for yy in both:
                to_core(j, yy).start()

    def tick(i, carry):
        @pl.when(i + ahead < chunks)
        def _():
            start_z(i + ahead, y)

            @pl.when(y_first(i + ahead))
            def _():
                from_over(i + ahead, z).wait_recv()
                start_z(i + ahead, 1 - y)

        @pl.when(jnp.logical_and(i + OVER_AHEAD < chunks, jnp.logical_not(y_first(i + OVER_AHEAD))))
        def _():
            to_over(i + OVER_AHEAD, z).start()

        for d in range(1, nz):
            j = i - d + 1

            @pl.when(jnp.logical_and(within(j), jnp.logical_not(y_first(j))))
            def _():
                stage(j, d, False)

            @pl.when(jnp.logical_and(within(j), y_first(j)))
            def _():
                stage(j, d, True)

        jy = i - nz + 1

        @pl.when(jnp.logical_and(within(jy), jnp.logical_not(y_first(jy))))
        def _():
            for zp in range(nz):
                from_over(jy, zp).wait_recv()
            to_core(jy, 1 - y).start()

        @pl.when(i == behind)
        def _():
            normalize_sources()

        @pl.when(i >= behind)
        def _():
            for yy in range(2):
                from_core(i - behind, yy).wait_recv()
            compute(i - behind)

        return carry

    lax.fori_loop(0, chunks + behind, tick, 0)

    def col_copy(k):
        other = lax.rem(s + k, ns)
        return remote(colbuf.at[other], colin.at[s], ksend.at[k], krecv.at[s], (other, t))

    for k in range(1, ns):
        col_copy(k).start()
    colin[s] = colbuf[s]


    best = lowest((8, rows))
    for k in range(4):
        flat = rowbest[k].T
        for q in range(128 // 8):
            best = insert(best, flat[q * 8 : (q + 1) * 8, :])
    rowbuf[...] = stacked(fold_sublanes(best))
    rowin[t] = rowbuf[...]

    def row_copy(k):
        other = lax.rem(t + k, nt)
        return remote(rowbuf, rowin.at[t], rsend.at[k], rrecv.at[t], (s, other))

    for k in range(1, nt):
        row_copy(k).start()

    for k in range(1, ns):
        other = lax.rem(s + k, ns)
        remote(colbuf.at[0], colin.at[other], ksend.at[k], krecv.at[other], (other, t)).wait_recv()
    best = lowest((8, ow))
    for p in range(ns):
        best = insert(best, colin[p])
    best = fold_sublanes(best)
    ktown[...] = (best[0] + best[1] + best[2] + best[3]) * 0.25

    def mean_copy(k):
        other = lax.rem(s + k, ns)
        return remote(ktown, ktin.at[s], msend.at[k], mrecv.at[s], (other, t))

    for k in range(1, ns):
        mean_copy(k).start()
    ktin[s] = ktown[...]

    for k in range(1, nt):
        other = lax.rem(t + k, nt)
        remote(rowbuf, rowin.at[other], rsend.at[k], rrecv.at[other], (s, other)).wait_recv()
    best = lowest((8, rows))
    for p in range(nt):
        best = insert(best, rowin[p])
    best = fold_sublanes(best)
    ks_out[...] = (best[0] + best[1] + best[2] + best[3]) * 0.25

    def drain(j, carry):
        def drain_z(zp, yy):
            @pl.when(jnp.logical_and(has_right, zp <= z))
            def _():
                to_right(j, zp, yy).wait_send()

            @pl.when(jnp.logical_and(has_left, zp >= z))
            def _():
                to_left(j, zp, yy).wait_send()

        for zp in range(nz):
            drain_z(zp, y)

        @pl.when(y_first(j))
        def _():
            for zp in range(nz):
                drain_z(zp, 1 - y)
            to_over(j, z).wait_send()

        @pl.when(jnp.logical_not(y_first(j)))
        def _():
            for zp in range(nz):
                to_over(j, zp).wait_send()

        for yy in range(2):
            to_core(j, yy).wait_send()
        return carry

    lax.fori_loop(0, chunks, drain, 0)
    for j in range(max(0, chunks - 2), chunks):
        out_copy(j).wait()
    for k in range(1, nt):
        to_tgt(k).wait_send()
        row_copy(k).wait_send()
    for k in range(1, ns):
        col_copy(k).wait_send()
        mean_copy(k).wait_send()
    for k in range(1, ns):
        other = lax.rem(s + k, ns)
        remote(ktown, ktin.at[other], msend.at[k], mrecv.at[other], (other, t)).wait_recv()
    kt_out[...] = ktin[...]


def body(ns, nt, src_emb, tgt_emb, src_ids, tgt_ids):
    rows, part = src_emb.shape
    cols, feats = tgt_emb.shape
    width = part * nt
    nz = ns // 4
    cw = min(CHUNK, cols)
    chunks = cols // cw
    ow = cols // ns
    f32, bf16 = jnp.float32, jnp.bfloat16
    dma = pltpu.SemaphoreType.DMA
    hbm = pl.BlockSpec(memory_space=pl.ANY)
    vmem = pl.BlockSpec(memory_space=pltpu.VMEM)
    scores, kt, ks = pl.pallas_call(
        functools.partial(kernel, (ns, nt, nz, chunks, cw, feats)),
        out_shape=(
            jax.ShapeDtypeStruct((rows, cols), f32),
            jax.ShapeDtypeStruct((ns, 8, ow), f32),
            jax.ShapeDtypeStruct((8, rows), f32),
        ),
        in_specs=[hbm, hbm, vmem, vmem],
        out_specs=(hbm, vmem, vmem),
        scratch_shapes=[
            pltpu.VMEM((rows, 128), jnp.int32),
            pltpu.VMEM((chunks, nz, 2, 2, feats, cw), bf16),
            pltpu.VMEM((rows, width), bf16),
            pltpu.VMEM((rows, width), bf16),
            pltpu.VMEM((width, cw), bf16),
            pltpu.VMEM((2, rows, cw), f32),
            pltpu.VMEM((4, rows, 128), f32),
            pltpu.VMEM((ns, 8, ow), f32),
            pltpu.VMEM((ns, 8, ow), f32),
            pltpu.VMEM((8, ow), f32),
            pltpu.VMEM((ns, 8, ow), f32),
            pltpu.VMEM((8, rows), f32),
            pltpu.VMEM((nt, 8, rows), f32),
            dma((chunks, nz, 2)),
            dma((2, chunks, nz, 2)),
            dma((chunks, nz)),
            dma((chunks, nz)),
            dma((chunks, 2)),
            dma((chunks, 2)),
            dma((nt,)),
            dma((nt,)),
            dma((nt,)),
            dma((nt,)),
            dma((ns,)),
            dma((ns,)),
            dma((ns,)),
            dma((ns,)),
            dma((1 + chunks,)),
            dma((2,)),
        ],
        compiler_params=pltpu.CompilerParams(
            collective_id=0, has_side_effects=True, vmem_limit_bytes=32 * 2**20
        ),
    )(tgt_emb.T, src_emb, src_ids.reshape(1, rows), tgt_ids.reshape(1, cols))
    knn_src = ks[0]
    knn_tgt = kt[:, 0, :].reshape(cols)
    ratio = scores / (0.5 * (knn_src[:, None] + knn_tgt[None, :]))
    return jnp.where(src_ids[:, None] == tgt_ids[None, :], jnp.float32(0.0), ratio)


def solution(mesh):
    return jax.shard_map(
        functools.partial(body, mesh.shape["src"], mesh.shape["tgt"]),
        mesh=mesh,
        in_specs=(P("src", "tgt"), P("tgt", "src"), P("src"), P("tgt")),
        out_specs=P("src", "tgt"),
        check_vma=False,
    )
```

profile of v0, /device:TPU:0, one launch (start us, length us, event | category | flops | bytes accessed | tf_op | source)
XLA Modules:
  0.0 81.7 jit_solution(15568201471112611753)
XLA Ops:
  0.0 0.0 copy-start
  0.0 1.0 %copy-done = bf16[4096,64]{0,1:T(8,128)(2,1)S(1)} copy-done((bf16[4096,64]{0,1:T(8,128)(2,1)S(1)}, bf16[4096,64]{0,1:T(8,128)(2,1)}, u32[]{:S(2)}) %copy-start) | copy-done | bytes 524312
  1.0 0.0 copy-start.1
  1.0 1.0 %copy-done.1 = bf16[512,512]{1,0:T(8,128)(2,1)S(1)} copy-done((bf16[512,512]{1,0:T(8,128)(2,1)S(1)}, bf16[512,512]{1,0:T(8,128)(2,1)}, u32[]{:S(2)}) %copy-start.1) | copy-done | bytes 524312
  2.1 0.0 copy-start.2
  2.1 0.7 copy-done.2
  2.8 0.0 copy-start.3
  2.8 0.7 copy-done.3
  3.5 73.7 %shard_map.46 = (f32[512,4096]{1,0:T(8,128)S(1)}, f32[16,8,256]{2,1,0:T(8,128)S(1)}, f32[8,512]{1,0:T(8,128)S(1)}) custom-call(bf16[64,4096]{1,0:T(8,128)(2,1)S(1)} %bitcast.5, bf16[512,512]{1,0:T(8,128)(2,1)S(1)} %copy-done.1, s32[1,512]{1,0:T(1,128)S(1)} %bitcast.7, s32[1,4096]{1,0:T(1,128)S(1)} %bitcast.6), custom_call_target="tpu_custom_call" | custom-call | tf_op jit(solution)/shard_map/pallas_call | solution.py:407
  77.2 4.5 %divide_select_fusion = f32[512,4096]{1,0:T(8,128)} fusion(f32[512,4096]{1,0:T(8,128)S(1)} %get-tuple-element.8, f32[4096]{0:T(1024)S(1)} %bitcast.8, f32[512]{0:T(512)S(1)} %bitcast.9, s32[4096]{0:T(1024)S(1)} %copy-done.2, s32[512]{0:T(512)S(1)} %copy-done.3), kind=kLoop, calls=%fused_computation | loop fusion | flops 10485760 | bytes 16814080 | tf_op jit(solution)/shard_map/jit(_where)/select_n | solution.py:454
  (2 shorter events, 0.0 us)
Async XLA Ops:
  0.0 1.0 %copy-start = (bf16[4096,64]{0,1:T(8,128)(2,1)S(1)}, bf16[4096,64]{0,1:T(8,128)(2,1)}, u32[]{:S(2)}) copy-start(bf16[4096,64]{0,1:T(8,128)(2,1)} %param.5) | copy-start | bytes 1572868
  1.0 1.0 %copy-start.1 = (bf16[512,512]{1,0:T(8,128)(2,1)S(1)}, bf16[512,512]{1,0:T(8,128)(2,1)}, u32[]{:S(2)}) copy-start(bf16[512,512]{1,0:T(8,128)(2,1)} %a_ref.1) | copy-start | bytes 1572868
  2.1 0.7 copy-start.2
  2.8 0.7 copy-start.3
where the time goes:
time: 82 us; the launch traced here: 81.7 us
  Pallas kernels  73.7 us (90%)
  other arithmetic  4.45 us (5%)
  local copies, waits for them, and re-layouts  3.49 us (4%)
    pallas_call x1, Pallas kernels, body(): pl.pallas_call(functools.partial(kernel, (ns, nt, nz, chunks, cw, feats))...  73.7 us
    select_n x1, other arithmetic, body(): jnp.where(src_ids[:, None] == tgt_ids[None, :], jnp.float32(0.0), ratio)  4.45 us
    unnamed x8, local copies, waits for them, and re-layouts  3.48 us

commit v1 on v0

v1 whole, which is shorter than its diff:
```python
import functools

import jax
import jax.numpy as jnp
from jax import lax
from jax.experimental import pallas as pl
from jax.experimental.pallas import tpu as pltpu
from jax.sharding import PartitionSpec as P

epsilon = 1e-06
excluded_score = -2.0
MESH = pl.DeviceIdType.MESH
CHUNK = 512
UNIT = 256
EVERY, EVERY_AT = 8, 7
Z_AHEAD = 4
Y_AHEAD = 6
BLOCK = 32
HOP = 1
Y_LAG = 1
CORE_LAG = 1
MERGE_LAG = 1


def sort4(v):
    a, b = jnp.maximum(v[0], v[1]), jnp.minimum(v[0], v[1])
    c, d = jnp.maximum(v[2], v[3]), jnp.minimum(v[2], v[3])
    top, e = jnp.maximum(a, c), jnp.minimum(a, c)
    f, low = jnp.maximum(b, d), jnp.minimum(b, d)
    return (top, jnp.maximum(e, f), jnp.minimum(e, f), low)


def merge(first, second):
    c = [jnp.maximum(first[k], second[3 - k]) for k in range(4)]
    a, b = jnp.maximum(c[0], c[2]), jnp.maximum(c[1], c[3])
    d, e = jnp.minimum(c[0], c[2]), jnp.minimum(c[1], c[3])
    return (jnp.maximum(a, b), jnp.minimum(a, b), jnp.maximum(d, e), jnp.minimum(d, e))


def insert(best, value):
    out = []
    for level in best[:-1]:
        out.append(jnp.maximum(level, value))
        value = jnp.minimum(level, value)
    out.append(jnp.maximum(best[-1], value))
    return tuple(out)


def absorb(best, values):
    whole = len(values) // 4 * 4
    for k in range(0, whole, 4):
        best = merge(best, sort4(values[k : k + 4]))
    for value in values[whole:]:
        best = insert(best, value)
    return best


def fold_sublanes(best, shifts=(4, 2, 1)):
    for shift in shifts:
        best = merge(best, tuple(pltpu.roll(level, shift, 0) for level in best))
    return best


def mean_of(best):
    return (best[0] + best[1] + best[2] + best[3]) * 0.25


def lowest(shape):
    return tuple(jnp.full(shape, -jnp.inf, jnp.float32) for _ in range(4))


def kernel(dims, x_ref, a_ref, sid_ref, tid_ref, s_out, kt_out, ks_out, sid, tid, sids, g, a_whole, a_unit, rowbest,
           colbuf, colin, tailin, ktown, rowbuf, rowin, zrecv, zsend, yrecv, ysend, crecv, csend, arecv, asend, rrecv,
           rsend, krecv, ksend, mrecv, msend, trecv, tsend, lsem):
    ns, nt, nz, chunks, cw, feats = dims
    s = lax.axis_index("src")
    t = lax.axis_index("tgt")
    z, y, c = s // 4, (s // 2) % 2, s % 2
    right = (s + 4, t)
    left = (s - 4, t)
    over = (z * 4 + (1 - y) * 2 + c, t)
    core = (s + 1 - 2 * c, t)
    rows, width = a_unit.shape
    part = a_ref.shape[1]
    per = cw // UNIT
    units = chunks * per
    split = units - per
    has_right, has_left = z + 1 < nz, z >= 1

    def remote(src, dst, send, recv, where):
        return pltpu.make_async_remote_copy(
            src_ref=src, dst_ref=dst, send_sem=send, recv_sem=recv, device_id=where, device_id_type=MESH
        )

    def chunk_cols(j):
        return pl.ds(pl.multiple_of(j * cw, cw), cw)

    barrier = pltpu.get_barrier_semaphore()

    @pl.when(has_right)
    def _():
        pl.semaphore_signal(barrier, inc=1, device_id=right, device_id_type=MESH)

    @pl.when(has_left)
    def _():
        pl.semaphore_signal(barrier, inc=1, device_id=left, device_id_type=MESH)

    pl.semaphore_signal(barrier, inc=1, device_id=over, device_id_type=MESH)
    pl.semaphore_signal(barrier, inc=1, device_id=core, device_id_type=MESH)
    for k in range(1, nt):
        pl.semaphore_signal(barrier, inc=1, device_id=(s, lax.rem(t + k, nt)), device_id_type=MESH)

    for j in range(chunks):
        pltpu.make_async_copy(x_ref.at[:, chunk_cols(j)], g.at[j, z, y, c], lsem.at[0]).start()
    acols = pl.ds(pl.multiple_of(t * part, part), part)
    local_a = pltpu.make_async_copy(a_ref, a_whole.at[:, acols], lsem.at[1])
    local_sid = pltpu.make_async_copy(sid_ref, sid, lsem.at[2])
    local_tid = pltpu.make_async_copy(tid_ref, tid, lsem.at[3])
    local_a.start()
    local_sid.start()
    local_tid.start()
    pl.semaphore_wait(barrier, 1 + nt + has_right.astype(jnp.int32) + has_left.astype(jnp.int32))

    firsts = [j for j in range(chunks) if j > 0 and j % EVERY == EVERY_AT]
    n_first, n_rest = len(firsts), chunks - len(firsts)

    def y_first(j):
        if isinstance(j, int):
            return j in firsts
        return jnp.logical_and(lax.rem(j, EVERY) == EVERY_AT, j > 0)

    def z_piece(j, zp, first):
        return g.at[j, zp, :, c] if first else g.at[j, zp, y, c]

    def to_right(j, zp, first, own=False):
        ref = z_piece(j, zp, first)
        src = x_ref.at[:, chunk_cols(j)] if own else ref
        return remote(src, ref, zsend.at[0, int(first), zp], zrecv.at[j, zp], right)

    def to_left(j, zp, first, own=False):
        ref = z_piece(j, zp, first)
        src = x_ref.at[:, chunk_cols(j)] if own else ref
        return remote(src, ref, zsend.at[1, int(first), zp], zrecv.at[j, zp], left)

    def to_over(j, zp, first, own=False):
        ref = g.at[j, zp, y, c]
        src = x_ref.at[:, chunk_cols(j)] if own else ref
        return remote(src, ref, ysend.at[int(first)], yrecv.at[j], over)

    def from_over(j, first):
        ref = g.at[j, z, 1 - y, c] if first else g.at[j, :, 1 - y, c]
        return remote(ref, ref, ysend.at[int(first)], yrecv.at[j], over)

    def to_core(j, yy):
        ref = g.at[j, :, yy, c]
        return remote(ref, ref, csend.at[0], crecv.at[j], core)

    def from_core(j):
        ref = g.at[j, :, :, 1 - c]
        return remote(ref, ref, csend.at[0], crecv.at[j], core)

    def start_side(j, first, to_side, there):
        @pl.when(there)
        def _():
            to_side(j, z, first, not first).start()

    def to_tgt(k):
        return remote(a_ref, a_whole.at[:, acols], asend.at[0], arecv.at[t], (s, lax.rem(t + k, nt)))

    z_ahead, y_ahead = min(Z_AHEAD, chunks), min(Y_AHEAD, chunks)
    depth = HOP * (nz - 1)
    for j in firsts:
        to_over(j, z, True, True).start()
    sides = ((to_left, has_left, HOP * z - depth), (to_right, has_right, -HOP * z))
    for j in range(max(y_ahead, z_ahead)):
        if j < y_ahead and j not in firsts:
            to_over(j, z, False, True).start()
        if j < z_ahead and j not in firsts:
            for to_side, there, lead in sides:
                start_side(j, False, to_side, jnp.logical_and(there, j < lead + z_ahead))
    for k in range(1, nt):
        to_tgt(k).start()
    pltpu.make_async_copy(g.at[:, z, y, c], g.at[:, z, y, c], lsem.at[0]).wait()
    for j in firsts:
        from_over(j, True).wait_recv()
        if j < z_ahead:
            for to_side, there, lead in sides:
                start_side(j, True, to_side, jnp.logical_and(there, j < lead + z_ahead))
    local_sid.wait()
    local_tid.wait()
    sids[...] = jnp.broadcast_to(sid[...], (128, rows)).T
    for k in range(4):
        rowbest[k] = jnp.full(rowbest.shape[1:], -jnp.inf, jnp.float32)

    def normalize_sources():
        local_a.wait()
        for k in range(1, nt):
            other = lax.rem(t + k, nt)
            cols = pl.ds(pl.multiple_of(other * part, part), part)
            remote(a_ref, a_whole.at[:, cols], asend.at[0], arecv.at[other], (s, other)).wait_recv()
        block = 16

        def step(r, carry):
            at = pl.ds(pl.multiple_of(r * block, block), block)
            v = a_whole[at, :].astype(jnp.float32)
            scale = jnp.sqrt(jnp.sum(v * v, axis=1, keepdims=True) + epsilon)
            a_unit[at, :] = (v / scale).astype(jnp.bfloat16)
            return carry

        lax.fori_loop(0, rows // block, step, 0, unroll=2)

    def compute(j):
        def squares(k, acc):
            v = g[j, k // 4, (k // 2) % 2, k % 2].astype(jnp.float32)
            return acc + jnp.sum((v * v).reshape(feats // 8, 8, cw), axis=0)

        acc = lax.fori_loop(0, ns, squares, jnp.zeros((8, cw), jnp.float32), unroll=2)
        inverse = jnp.broadcast_to(1.0 / jnp.sqrt(jnp.sum(acc, axis=0, keepdims=True) + epsilon), (8, cw))
        cols = chunk_cols(j)
        s_out[:, cols] = jnp.dot(a_unit[...], g[j].reshape(width, cw), preferred_element_type=jnp.float32)
        tids = jnp.broadcast_to(tid[:, cols], (8, cw))
        lanes = cw // 128

        def group(r, best):
            found = []
            for h in range(4):
                at = pl.ds(pl.multiple_of(r * 32 + h * 8, 8), 8)
                ids = sids[at, :]
                pieces = []
                for q in range(lanes):
                    span = slice(q * 128, (q + 1) * 128)
                    where = pl.ds(pl.multiple_of(j * cw + q * 128, 128), 128)
                    v = jnp.where(ids == tids[:, span], jnp.float32(excluded_score), s_out[at, where] * inverse[:, span])
                    s_out[at, where] = v
                    pieces.append(v)
                row = absorb(tuple(rowbest[k, at, :] for k in range(4)), pieces)
                for k in range(4):
                    rowbest[k, at, :] = row[k]
                found.append(pieces)
            return tuple(absorb(best[q], [found[h][q] for h in range(4)]) for q in range(lanes))

        best = lax.fori_loop(0, rows // 32, group, tuple(lowest((8, 128)) for _ in range(lanes)))
        row = lax.broadcasted_iota(jnp.int32, (8, 128), 0)
        for u in range(per):
            half = [fold_sublanes(best[u * (UNIT // 128) + q]) for q in range(UNIT // 128)]
            out = half[0][0]
            for q in range(2):
                for k in range(4):
                    out = jnp.where(row == q * 4 + k, half[q][k], out)
            colbuf[j * per + u] = out

    def col_copy(u, k):
        return remote(colbuf.at[u], colin.at[s], ksend.at[0], krecv.at[0], (u, t))

    def send_columns(j):
        for u in range(per):
            unit = j * per + u

            @pl.when(s != unit)
            def _():
                col_copy(unit, 0).start()

            @pl.when(s == unit)
            def _():
                colin[s] = colbuf[unit]

    def knn_of(pieces):
        best = absorb(lowest((8, 128)), pieces)
        return mean_of(fold_sublanes(best, (2, 1)))

    def mean_copy(k):
        return remote(ktown, kt_out.at[s], msend.at[0], mrecv.at[0], (lax.rem(s + k, ns), t))

    def merge_columns(j):
        @pl.when(s // per == j)
        def _():
            ref = colin.at[pl.ds(0, ns - 1)]
            remote(ref, ref, ksend.at[0], krecv.at[0], core).wait_recv()
            ktown[...] = knn_of([colin[p] for p in range(ns)])
            for k in range(1, ns):
                mean_copy(k).start()
            kt_out[s] = ktown[...]

    def within(j):
        return jnp.logical_and(j >= 0, j < chunks)

    def relay(to_side, there, behind_me, j, first):
        for d in range(nz - 1, 0, -1):
            zp, present = behind_me(d)

            @pl.when(present)
            def _():
                to_side(j, zp, first).wait_recv()

                @pl.when(there)
                def _():
                    to_side(j, zp, first).start()

                if not first:
                    to_over(j, zp, False).start()

    relays = (
        functools.partial(relay, to_left, has_left, lambda d: (z + d, z + d < nz)),
        functools.partial(relay, to_right, has_right, lambda d: (z - d, z - d >= 0)),
    )

    def pass_on(j, first):
        to_core(j, y).start()
        if first:
            to_core(j, 1 - y).start()

    y_behind = depth + Y_LAG
    behind = y_behind + CORE_LAG

    def either(j, what):
        @pl.when(jnp.logical_and(within(j), jnp.logical_not(y_first(j))))
        def _():
            what(j, False)

        if n_first:

            @pl.when(jnp.logical_and(within(j), y_first(j)))
            def _():
                what(j, True)

    def tick(i, carry):
        for (to_side, there, lead), relay_side in zip(sides, relays):
            j = i + lead
            either(j + z_ahead, lambda j, first: start_side(j, first, to_side, there))
            either(j, relay_side)

        j = i - depth + y_ahead

        @pl.when(jnp.logical_and(j >= y_ahead, jnp.logical_and(j < chunks, jnp.logical_not(y_first(j)))))
        def _():
            to_over(j, z, False, True).start()

        either(i - depth, pass_on)

        jy = i - y_behind

        @pl.when(jnp.logical_and(within(jy), jnp.logical_not(y_first(jy))))
        def _():
            from_over(jy, False).wait_recv()
            to_core(jy, 1 - y).start()

        jc = i - behind

        @pl.when(jc == 0)
        def _():
            normalize_sources()

        @pl.when(jc >= 0)
        def _():
            from_core(jc).wait_recv()
            compute(jc)


        @pl.when(jnp.logical_and(jc >= 0, jc < chunks - 1))
        def _():
            send_columns(jc)

        @pl.when(jnp.logical_and(jc >= MERGE_LAG, jc < chunks - 1))
        def _():
            merge_columns(jc - MERGE_LAG)

        return carry

    lax.fori_loop(0, chunks + behind, tick, 0)

    def tail_copy(k):
        mine = tailin.at[s]
        return remote(colbuf.at[pl.ds(split, per)], mine, tsend.at[0], trecv.at[0], (lax.rem(s + k, ns), t))

    def row_copy(k):
        return remote(rowbuf, rowin.at[t], rsend.at[0], rrecv.at[0], (s, lax.rem(t + k, nt)))

    for k in range(1, ns):
        tail_copy(k).start()
    tailin[s] = colbuf[pl.ds(split, per)]
    for j in range(max(0, chunks - 1 - MERGE_LAG), chunks - 1):
        merge_columns(j)
    flat = [rowbest[k].T for k in range(4)]
    best = lowest((8, rows))
    for q in range(128 // 8):
        best = merge(best, tuple(flat[k][q * 8 : (q + 1) * 8, :] for k in range(4)))
    best = fold_sublanes(best)
    row = lax.broadcasted_iota(jnp.int32, (8, rows), 0)
    out = jnp.full((8, rows), -jnp.inf, jnp.float32)
    for k in range(4):
        out = jnp.where(row == k, best[k], out)
    rowbuf[...] = out
    rowin[t] = out
    for k in range(1, nt):
        row_copy(k).start()

    def drain_z(zp, first, count):
        ref = g.at[pl.ds(0, count), 0, :, 0] if first else g.at[pl.ds(0, count), 0, 0, 0]

        @pl.when(jnp.logical_and(has_right, zp <= z))
        def _():
            remote(ref, ref, zsend.at[0, int(first), zp], zrecv.at[0, zp], right).wait_send()

        @pl.when(jnp.logical_and(has_left, zp >= z))
        def _():
            remote(ref, ref, zsend.at[1, int(first), zp], zrecv.at[0, zp], left).wait_send()

    for zp in range(nz):
        drain_z(zp, False, n_rest)
        if n_first:
            drain_z(zp, True, n_first)
    ref = g.at[pl.ds(0, n_rest), :, 0, 0]
    remote(ref, ref, ysend.at[0], yrecv.at[0], over).wait_send()
    if n_first:
        ref = g.at[pl.ds(0, n_first), 0, 0, 0]
        remote(ref, ref, ysend.at[1], yrecv.at[0], over).wait_send()
    ref = g.at[:, :, :, c]
    remote(ref, ref, csend.at[0], crecv.at[0], core).wait_send()
    for k in range(1, nt):
        to_tgt(k).wait_send()

    ref = tailin.at[pl.ds(0, ns - 1)]
    remote(ref, ref, tsend.at[0], trecv.at[0], core).wait_recv()
    for u in range(per):
        kt_out[split + u] = knn_of([tailin[p, u] for p in range(ns)])
    for k in range(1, nt):
        row_copy(k).wait_send()
    ref = rowin.at[pl.ds(0, nt - 1)]
    remote(ref, ref, rsend.at[0], rrecv.at[0], core).wait_recv()
    half = 0.5 * mean_of(fold_sublanes(absorb(lowest((8, rows)), [rowin[p] for p in range(nt)])))
    ks_out[...] = jnp.broadcast_to(half[0:1], (128, rows)).T

    @pl.when(s < split)
    def _():
        ref = colbuf.at[pl.ds(0, split - 1)]
        remote(ref, ref, ksend.at[0], krecv.at[0], core).wait_send()
        mean = kt_out.at[pl.ds(0, split - 1)]
        remote(mean, mean, msend.at[0], mrecv.at[0], core).wait_recv()
        for k in range(1, ns):
            mean_copy(k).wait_send()

    @pl.when(s >= split)
    def _():
        ref = colbuf.at[pl.ds(0, split)]
        remote(ref, ref, ksend.at[0], krecv.at[0], core).wait_send()
        mean = kt_out.at[pl.ds(0, split)]
        remote(mean, mean, msend.at[0], mrecv.at[0], core).wait_recv()

    ref = tailin.at[pl.ds(0, ns - 1)]
    remote(ref, ref, tsend.at[0], trecv.at[0], core).wait_send()


def finish(s_ref, kt_ref, ks_ref, out_ref, half, held, sem):
    rows, cols = s_ref.shape
    tiles = cols // 128
    for u in range(tiles // 2):
        for q in range(2):
            half[2 * u + q] = jnp.broadcast_to(0.5 * kt_ref[u, 4 * q + 3 : 4 * q + 4, :], (8, 128))

    def block(b, carry):
        def at(h):
            return pl.ds(pl.multiple_of(b * BLOCK + 8 * h, 8), 8)

        mine = [ks_ref[at(h), :] for h in range(BLOCK // 8)]

        def tile(q, carry):
            lanes = pl.ds(pl.multiple_of(q * 128, 128), 128)
            other = half[q]
            for h in range(BLOCK // 8):
                v = s_ref[at(h), lanes]
                held[at(h), lanes] = jnp.where(v == excluded_score, jnp.float32(0.0), v / (mine[h] + other))
            return carry

        lax.fori_loop(0, tiles, tile, 0, unroll=4)
        span = pl.ds(pl.multiple_of(b * BLOCK, BLOCK), BLOCK)
        pltpu.make_async_copy(held.at[span], out_ref.at[span], sem.at[0]).start()
        return carry

    lax.fori_loop(0, rows // BLOCK, block, 0)
    pltpu.make_async_copy(held, out_ref, sem.at[0]).wait()


def body(ns, nt, src_emb, tgt_emb, src_ids, tgt_ids):
    rows, part = src_emb.shape
    cols, feats = tgt_emb.shape
    width = part * nt
    nz = ns // 4
    cw = min(CHUNK, cols)
    chunks = cols // cw
    units = cols // UNIT
    f32, bf16 = jnp.float32, jnp.bfloat16
    dma = pltpu.SemaphoreType.DMA
    hbm = pl.BlockSpec(memory_space=pltpu.MemorySpace.HBM)
    vmem = pl.BlockSpec(memory_space=pltpu.VMEM)
    args = (tgt_emb.T, src_emb, src_ids.reshape(1, rows), tgt_ids.reshape(1, cols))
    scores, kt, ks = pl.pallas_call(
        functools.partial(kernel, (ns, nt, nz, chunks, cw, feats)),
        out_shape=(
            jax.ShapeDtypeStruct((rows, cols), f32),
            jax.ShapeDtypeStruct((units, 8, 128), f32),
            jax.ShapeDtypeStruct((rows, 128), f32),
        ),
        in_specs=[hbm, hbm, hbm, hbm],
        out_specs=(vmem, vmem, vmem),
        scratch_shapes=[
            pltpu.VMEM((1, rows), jnp.int32),
            pltpu.VMEM((1, cols), jnp.int32),
            pltpu.VMEM((rows, 128), jnp.int32),
            pltpu.VMEM((chunks, nz, 2, 2, feats, cw), bf16),
            pltpu.VMEM((rows, width), bf16),
            pltpu.VMEM((rows, width), bf16),
            pltpu.VMEM((4, rows, 128), f32),
            pltpu.VMEM((units, 8, 128), f32),
            pltpu.VMEM((ns, 8, 128), f32),
            pltpu.VMEM((ns, cw // UNIT, 8, 128), f32),
            pltpu.VMEM((8, 128), f32),
            pltpu.VMEM((8, rows), f32),
            pltpu.VMEM((nt, 8, rows), f32),
            dma((chunks, nz)),
            dma((2, 2, nz)),
            dma((chunks,)),
            dma((2,)),
            dma((chunks,)),
            dma((1,)),
            dma((nt,)),
            dma((1,)),
            dma((1,)),
            dma((1,)),
            dma((1,)),
            dma((1,)),
            dma((1,)),
            dma((1,)),
            dma((1,)),
            dma((1,)),
            dma((4,)),
        ],
        compiler_params=pltpu.CompilerParams(
            collective_id=0, has_side_effects=True, vmem_limit_bytes=40 * 2**20
        ),
    )(*(pltpu.with_memory_space_constraint(v, pltpu.MemorySpace.HBM) for v in args))
    return pl.pallas_call(
        finish,
        out_shape=jax.ShapeDtypeStruct((rows, cols), f32),
        in_specs=[vmem, vmem, vmem],
        out_specs=pl.BlockSpec(memory_space=pl.ANY),
        scratch_shapes=[
            pltpu.VMEM((cols // 128, 8, 128), f32),
            pltpu.VMEM((rows, cols), f32),
            dma((1,)),
        ],
        compiler_params=pltpu.CompilerParams(vmem_limit_bytes=40 * 2**20),
    )(scores, kt, ks)


def solution(mesh):
    return jax.shard_map(
        functools.partial(body, mesh.shape["src"], mesh.shape["tgt"]),
        mesh=mesh,
        in_specs=(P("src", "tgt"), P("tgt", "src"), P("src"), P("tgt")),
        out_specs=P("src", "tgt"),
        check_vma=False,
    )
```

time: 82 us -> 73 us (0.89)
  other arithmetic: 4.45 us -> 0 us
  local copies, waits for them, and re-layouts: 3.49 us -> 0 us
    pallas_call x1, Pallas kernels: 73.7 us -> 68.3 us  [body(): pl.pallas_call(functools.partial(kernel, (ns, nt, nz, chunks, cw, feats))...]
    pallas_call x0 -> x1, Pallas kernels: none -> 4.56 us  [body(): pl.pallas_call(finish, out_shape=jax.ShapeDtypeStruct((rows, cols), f32),...]
    select_n x1 -> x0, other arithmetic: 4.45 us -> none  [body(): jnp.where(src_ids[:, None] == tgt_ids[None, :], jnp.float32(0.0), ratio)]
    unnamed x8 -> x0, local copies, waits for them, and re-layouts: 3.48 us -> none
where the time goes in v1:
time: 73 us; the launch traced here: 72.9 us
  Pallas kernels  72.9 us (100%)
    pallas_call x1, Pallas kernels, body(): pl.pallas_call(functools.partial(kernel, (ns, nt, nz, chunks, cw, feats))...  68.3 us
    pallas_call x1, Pallas kernels, body(): pl.pallas_call(finish, out_shape=jax.ShapeDtypeStruct((rows, cols), f32),...  4.56 us

profile of v1, /device:TPU:0, one launch (start us, length us, event | category | flops | bytes accessed | tf_op | source)
XLA Modules:
  0.0 72.9 jit_solution(14214437555496882682)
XLA Ops:
  0.0 68.3 %shard_map.46 = (f32[512,4096]{1,0:T(8,128)S(1)}, f32[16,8,128]{2,1,0:T(8,128)S(1)}, f32[512,128]{1,0:T(8,128)S(1)}) custom-call(bf16[64,4096]{1,0:T(8,128)(2,1)} %bitcast.3, bf16[512,512]{1,0:T(8,128)(2,1)} %a_ref.1, s32[1,512]{1,0:T(1,128)} %bitcast.5, s32[1,4096]{1,0:T(1,128)} %bitcast.4), custom_call_target="tpu_custom_call" | custom-call | tf_op jit(solution)/shard_map/pallas_call | solution.py:496
  68.3 4.6 %shard_map.47 = f32[512,4096]{1,0:T(8,128)} custom-call(f32[512,4096]{1,0:T(8,128)S(1)} %get-tuple-element.8.s_ref, f32[16,8,128]{2,1,0:T(8,128)S(1)} %get-tuple-element.9.kt_ref, f32[512,128]{1,0:T(8,128)S(1)} %get-tuple-element.10.ks_ref), custom_call_target="tpu_custom_call" | custom-call | tf_op jit(solution)/shard_map/pallas_call | solution.py:541

commit v2 on v1

--- a/solution.py
+++ b/solution.py
@@ -11,15 +11,13 @@
 excluded_score = -2.0
 MESH = pl.DeviceIdType.MESH
 CHUNK = 512
-UNIT = 256
-EVERY, EVERY_AT = 8, 7
-Z_AHEAD = 4
-Y_AHEAD = 6
+SWAP = False
+Z_AHEAD = 3
+Y_AHEAD = 7
 BLOCK = 32
 HOP = 1
-Y_LAG = 1
+Y_LAG = 2
 CORE_LAG = 1
-MERGE_LAG = 1
 
 
 def sort4(v):
@@ -82,9 +80,10 @@
     core = (s + 1 - 2 * c, t)
     rows, width = a_unit.shape
     part = a_ref.shape[1]
-    per = cw // UNIT
-    units = chunks * per
-    split = units - per
+    lanes = cw // 128
+    first = chunks - 1
+    early, last = (first, first - 1) if SWAP else (first - 1, first)
+    stride = ns // chunks
     has_right, has_left = z + 1 < nz, z >= 1
 
     def remote(src, dst, send, recv, where):
@@ -121,35 +120,34 @@
     local_tid.start()
     pl.semaphore_wait(barrier, 1 + nt + has_right.astype(jnp.int32) + has_left.astype(jnp.int32))
 
-    firsts = [j for j in range(chunks) if j > 0 and j % EVERY == EVERY_AT]
-    n_first, n_rest = len(firsts), chunks - len(firsts)
-
-    def y_first(j):
-        if isinstance(j, int):
-            return j in firsts
-        return jnp.logical_and(lax.rem(j, EVERY) == EVERY_AT, j > 0)
-
-    def z_piece(j, zp, first):
-        return g.at[j, zp, :, c] if first else g.at[j, zp, y, c]
-
-    def to_right(j, zp, first, own=False):
-        ref = z_piece(j, zp, first)
-        src = x_ref.at[:, chunk_cols(j)] if own else ref
-        return remote(src, ref, zsend.at[0, int(first), zp], zrecv.at[j, zp], right)
-
-    def to_left(j, zp, first, own=False):
-        ref = z_piece(j, zp, first)
-        src = x_ref.at[:, chunk_cols(j)] if own else ref
-        return remote(src, ref, zsend.at[1, int(first), zp], zrecv.at[j, zp], left)
-
-    def to_over(j, zp, first, own=False):
+    def to_right(j, zp, own=False):
+        ref = g.at[j, zp, y, c]
+        return remote(x_ref.at[:, chunk_cols(j)] if own else ref, ref, zsend.at[0, 0, zp], zrecv.at[j, zp], right)
+
+    def to_left(j, zp, own=False):
+        ref = g.at[j, zp, y, c]
+        return remote(x_ref.at[:, chunk_cols(j)] if own else ref, ref, zsend.at[1, 0, zp], zrecv.at[j, zp], left)
+
+    def both_right(zp):
+        ref = g.at[first, zp, :, c]
+        return remote(ref, ref, zsend.at[0, 1, zp], zrecv.at[first, zp], right)
+
+    def both_left(zp):
+        ref = g.at[first, zp, :, c]
+        return remote(ref, ref, zsend.at[1, 1, zp], zrecv.at[first, zp], left)
+
+    def to_over(j, zp, own=False):
         ref = g.at[j, zp, y, c]
         src = x_ref.at[:, chunk_cols(j)] if own else ref
-        return remote(src, ref, ysend.at[int(first)], yrecv.at[j], over)
-
-    def from_over(j, first):
-        ref = g.at[j, z, 1 - y, c] if first else g.at[j, :, 1 - y, c]
-        return remote(ref, ref, ysend.at[int(first)], yrecv.at[j], over)
+        return remote(src, ref, ysend.at[0], yrecv.at[j], over)
+
+    def from_over(j):
+        ref = g.at[j, :, 1 - y, c]
+        return remote(ref, ref, ysend.at[0], yrecv.at[j], over)
+
+    def swap(own):
+        ref = g.at[first, z, y, c] if own else g.at[first, z, 1 - y, c]
+        return remote(x_ref.at[:, chunk_cols(first)] if own else ref, ref, ysend.at[1], yrecv.at[first], over)
 
     def to_core(j, yy):
         ref = g.at[j, :, yy, c]
@@ -159,33 +157,27 @@
         ref = g.at[j, :, :, 1 - c]
         return remote(ref, ref, csend.at[0], crecv.at[j], core)
 
-    def start_side(j, first, to_side, there):
-        @pl.when(there)
-        def _():
-            to_side(j, z, first, not first).start()
-
     def to_tgt(k):
         return remote(a_ref, a_whole.at[:, acols], asend.at[0], arecv.at[t], (s, lax.rem(t + k, nt)))
 
-    z_ahead, y_ahead = min(Z_AHEAD, chunks), min(Y_AHEAD, chunks)
+    z_ahead, y_ahead = min(Z_AHEAD, first - 1), min(Y_AHEAD, first)
     depth = HOP * (nz - 1)
-    for j in firsts:
-        to_over(j, z, True, True).start()
     sides = ((to_left, has_left, HOP * z - depth), (to_right, has_right, -HOP * z))
+    swap(True).start()
     for j in range(max(y_ahead, z_ahead)):
-        if j < y_ahead and j not in firsts:
-            to_over(j, z, False, True).start()
-        if j < z_ahead and j not in firsts:
+        if j < y_ahead:
+            to_over(j, z, True).start()
+        if j < z_ahead:
             for to_side, there, lead in sides:
-                start_side(j, False, to_side, jnp.logical_and(there, j < lead + z_ahead))
+
+                @pl.when(jnp.logical_and(there, j < lead + z_ahead))
+                def _():
+                    to_side(j, z, True).start()
+
     for k in range(1, nt):
         to_tgt(k).start()
     pltpu.make_async_copy(g.at[:, z, y, c], g.at[:, z, y, c], lsem.at[0]).wait()
-    for j in firsts:
-        from_over(j, True).wait_recv()
-        if j < z_ahead:
-            for to_side, there, lead in sides:
-                start_side(j, True, to_side, jnp.logical_and(there, j < lead + z_ahead))
+    swap(False).wait_recv()
     local_sid.wait()
     local_tid.wait()
     sids[...] = jnp.broadcast_to(sid[...], (128, rows)).T
@@ -210,16 +202,13 @@
         lax.fori_loop(0, rows // block, step, 0, unroll=2)
 
     def compute(j):
-        def squares(k, acc):
-            v = g[j, k // 4, (k // 2) % 2, k % 2].astype(jnp.float32)
-            return acc + jnp.sum((v * v).reshape(feats // 8, 8, cw), axis=0)
-
-        acc = lax.fori_loop(0, ns, squares, jnp.zeros((8, cw), jnp.float32), unroll=2)
+        cols = chunk_cols(j)
+        found = g[j].reshape(width, cw)
+        s_out[:, cols] = jnp.dot(a_unit[...], found, preferred_element_type=jnp.float32)
+        found = found.astype(jnp.float32)
+        acc = jnp.sum((found * found).reshape(width // 8, 8, cw), axis=0)
         inverse = jnp.broadcast_to(1.0 / jnp.sqrt(jnp.sum(acc, axis=0, keepdims=True) + epsilon), (8, cw))
-        cols = chunk_cols(j)
-        s_out[:, cols] = jnp.dot(a_unit[...], g[j].reshape(width, cw), preferred_element_type=jnp.float32)
         tids = jnp.broadcast_to(tid[:, cols], (8, cw))
-        lanes = cw // 128
 
         def group(r, best):
             found = []
@@ -240,146 +229,165 @@
             return tuple(absorb(best[q], [found[h][q] for h in range(4)]) for q in range(lanes))
 
         best = lax.fori_loop(0, rows // 32, group, tuple(lowest((8, 128)) for _ in range(lanes)))
+        best = [fold_sublanes(b) for b in best]
         row = lax.broadcasted_iota(jnp.int32, (8, 128), 0)
-        for u in range(per):
-            half = [fold_sublanes(best[u * (UNIT // 128) + q]) for q in range(UNIT // 128)]
-            out = half[0][0]
-            for q in range(2):
-                for k in range(4):
-                    out = jnp.where(row == q * 4 + k, half[q][k], out)
-            colbuf[j * per + u] = out
-
-    def col_copy(u, k):
-        return remote(colbuf.at[u], colin.at[s], ksend.at[0], krecv.at[0], (u, t))
+        tiles = []
+        for q in range(0, lanes, 2):
+            out = best[q][0]
+            for k in range(1, 8):
+                out = jnp.where(row == k, best[q + k // 4][k % 4], out)
+            tiles.append(out)
+        colbuf[j] = jnp.concatenate(tiles, axis=0).astype(jnp.bfloat16)
 
     def send_columns(j):
-        for u in range(per):
-            unit = j * per + u
-
-            @pl.when(s != unit)
-            def _():
-                col_copy(unit, 0).start()
-
-            @pl.when(s == unit)
-            def _():
-                colin[s] = colbuf[unit]
-
-    def knn_of(pieces):
-        best = absorb(lowest((8, 128)), pieces)
-        return mean_of(fold_sublanes(best, (2, 1)))
+        owner = j * stride
+
+        @pl.when(s != owner)
+        def _():
+            remote(colbuf.at[j], colin.at[s], ksend.at[0], krecv.at[0], (owner, t)).start()
+
+        @pl.when(s == owner)
+        def _():
+            colin[s] = colbuf[j]
+
+    def knn_of(ref):
+        best = absorb(lowest((4 * lanes, 128)), [ref[p].astype(jnp.float32) for p in range(ns)])
+        mean = mean_of(fold_sublanes(best, (2, 1)))
+        return jnp.concatenate([mean[4 * q + 3 : 4 * q + 4] for q in range(lanes)], axis=0)
 
     def mean_copy(k):
-        return remote(ktown, kt_out.at[s], msend.at[0], mrecv.at[0], (lax.rem(s + k, ns), t))
+        j = s // stride
+        return remote(ktown, kt_out.at[j], msend.at[0], mrecv.at[0], (lax.rem(s + k, ns), t))
 
     def merge_columns(j):
-        @pl.when(s // per == j)
+        @pl.when(s == j * stride)
         def _():
             ref = colin.at[pl.ds(0, ns - 1)]
             remote(ref, ref, ksend.at[0], krecv.at[0], core).wait_recv()
-            ktown[...] = knn_of([colin[p] for p in range(ns)])
+            ktown[...] = knn_of(colin)
             for k in range(1, ns):
                 mean_copy(k).start()
-            kt_out[s] = ktown[...]
+            kt_out[j] = ktown[...]
 
     def within(j):
-        return jnp.logical_and(j >= 0, j < chunks)
-
-    def relay(to_side, there, behind_me, j, first):
-        for d in range(nz - 1, 0, -1):
+        return jnp.logical_and(j >= 0, j < first)
+
+    def relay(to_side, there, behind_me, j):
+        for d in range(1, nz):
             zp, present = behind_me(d)
 
             @pl.when(present)
             def _():
-                to_side(j, zp, first).wait_recv()
+                to_side(j, zp).wait_recv()
 
                 @pl.when(there)
                 def _():
-                    to_side(j, zp, first).start()
-
-                if not first:
-                    to_over(j, zp, False).start()
+                    to_side(j, zp).start()
+
+                to_over(j, zp).start()
 
     relays = (
         functools.partial(relay, to_left, has_left, lambda d: (z + d, z + d < nz)),
         functools.partial(relay, to_right, has_right, lambda d: (z - d, z - d >= 0)),
     )
 
-    def pass_on(j, first):
-        to_core(j, y).start()
-        if first:
-            to_core(j, 1 - y).start()
+    def relay_both(both, there, behind_me):
+        for d in range(1, nz):
+            zp, present = behind_me(d)
+
+            @pl.when(present)
+            def _():
+                both(zp).wait_recv()
+
+                @pl.when(there)
+                def _():
+                    both(zp).start()
+
+    relays_both = (
+        functools.partial(relay_both, both_left, has_left, lambda d: (z + d, z + d < nz)),
+        functools.partial(relay_both, both_right, has_right, lambda d: (z - d, z - d >= 0)),
+    )
 
     y_behind = depth + Y_LAG
     behind = y_behind + CORE_LAG
 
-    def either(j, what):
-        @pl.when(jnp.logical_and(within(j), jnp.logical_not(y_first(j))))
-        def _():
-            what(j, False)
-
-        if n_first:
-
-            @pl.when(jnp.logical_and(within(j), y_first(j)))
+    def tick(i, carry):
+        for (to_side, there, lead), both, relay_side, relay_pair in zip(sides, (both_left, both_right), relays, relays_both):
+            j = i + lead
+
+            @pl.when(jnp.logical_and(j + z_ahead == first, there))
             def _():
-                what(j, True)
-
-    def tick(i, carry):
-        for (to_side, there, lead), relay_side in zip(sides, relays):
-            j = i + lead
-            either(j + z_ahead, lambda j, first: start_side(j, first, to_side, there))
-            either(j, relay_side)
-
-        j = i - depth + y_ahead
-
-        @pl.when(jnp.logical_and(j >= y_ahead, jnp.logical_and(j < chunks, jnp.logical_not(y_first(j)))))
-        def _():
-            to_over(j, z, False, True).start()
-
-        either(i - depth, pass_on)
+                both(z).start()
+
+            @pl.when(j == first)
+            def _():
+                relay_pair()
+
+            @pl.when(jnp.logical_and(within(j + z_ahead), there))
+            def _():
+                to_side(j + z_ahead, z, True).start()
+
+            @pl.when(within(j))
+            def _():
+                relay_side(j)
+
+        j = i - depth
+
+        @pl.when(jnp.logical_and(j >= 0, j + y_ahead < first))
+        def _():
+            to_over(j + y_ahead, z, True).start()
+
+        @pl.when(within(j))
+        def _():
+            to_core(j, y).start()
+
+        @pl.when(j == first)
+        def _():
+            to_core(first, y).start()
+            to_core(first, 1 - y).start()
 
         jy = i - y_behind
 
-        @pl.when(jnp.logical_and(within(jy), jnp.logical_not(y_first(jy))))
-        def _():
-            from_over(jy, False).wait_recv()
+        @pl.when(within(jy))
+        def _():
+            from_over(jy).wait_recv()
             to_core(jy, 1 - y).start()
 
-        jc = i - behind
-
-        @pl.when(jc == 0)
+        m = i - behind
+        jc = jnp.where(m == first - 1, early, jnp.where(m == first, last, m))
+
+        @pl.when(m == 0)
         def _():
             normalize_sources()
 
-        @pl.when(jc >= 0)
+        @pl.when(m >= 0)
         def _():
             from_core(jc).wait_recv()
             compute(jc)
 
 
-        @pl.when(jnp.logical_and(jc >= 0, jc < chunks - 1))
+        @pl.when(jnp.logical_and(m >= 0, m < first))
         def _():
             send_columns(jc)
 
-        @pl.when(jnp.logical_and(jc >= MERGE_LAG, jc < chunks - 1))
-        def _():
-            merge_columns(jc - MERGE_LAG)
+        @pl.when(jnp.logical_and(m >= 1, m < first))
+        def _():
+            merge_columns(m - 1)
 
         return carry
 
     lax.fori_loop(0, chunks + behind, tick, 0)
 
     def tail_copy(k):
-        mine = tailin.at[s]
-        return remote(colbuf.at[pl.ds(split, per)], mine, tsend.at[0], trecv.at[0], (lax.rem(s + k, ns), t))
+        return remote(colbuf.at[last], tailin.at[s], tsend.at[0], trecv.at[0], (lax.rem(s + k, ns), t))
 
     def row_copy(k):
         return remote(rowbuf, rowin.at[t], rsend.at[0], rrecv.at[0], (s, lax.rem(t + k, nt)))
 
     for k in range(1, ns):
         tail_copy(k).start()
-    tailin[s] = colbuf[pl.ds(split, per)]
-    for j in range(max(0, chunks - 1 - MERGE_LAG), chunks - 1):
-        merge_columns(j)
+    tailin[s] = colbuf[last]
+    merge_columns(early)
     flat = [rowbest[k].T for k in range(4)]
     best = lowest((8, rows))
     for q in range(128 // 8):
@@ -394,26 +402,21 @@
     for k in range(1, nt):
         row_copy(k).start()
 
-    def drain_z(zp, first, count):
-        ref = g.at[pl.ds(0, count), 0, :, 0] if first else g.at[pl.ds(0, count), 0, 0, 0]
-
+    def drain_z(zp, kind, ref):
         @pl.when(jnp.logical_and(has_right, zp <= z))
         def _():
-            remote(ref, ref, zsend.at[0, int(first), zp], zrecv.at[0, zp], right).wait_send()
+            remote(ref, ref, zsend.at[0, kind, zp], zrecv.at[0, zp], right).wait_send()
 
         @pl.when(jnp.logical_and(has_left, zp >= z))
         def _():
-            remote(ref, ref, zsend.at[1, int(first), zp], zrecv.at[0, zp], left).wait_send()
+            remote(ref, ref, zsend.at[1, kind, zp], zrecv.at[0, zp], left).wait_send()
 
     for zp in range(nz):
-        drain_z(zp, False, n_rest)
-        if n_first:
-            drain_z(zp, True, n_first)
-    ref = g.at[pl.ds(0, n_rest), :, 0, 0]
+        drain_z(zp, 0, g.at[pl.ds(0, first), 0, 0, 0])
+        drain_z(zp, 1, g.at[0, 0, :, 0])
+    ref = g.at[pl.ds(0, first), :, 0, 0]
     remote(ref, ref, ysend.at[0], yrecv.at[0], over).wait_send()
-    if n_first:
-        ref = g.at[pl.ds(0, n_first), 0, 0, 0]
-        remote(ref, ref, ysend.at[1], yrecv.at[0], over).wait_send()
+    swap(True).wait_send()
     ref = g.at[:, :, :, c]
     remote(ref, ref, csend.at[0], crecv.at[0], core).wait_send()
     for k in range(1, nt):
@@ -421,8 +424,7 @@
 
     ref = tailin.at[pl.ds(0, ns - 1)]
     remote(ref, ref, tsend.at[0], trecv.at[0], core).wait_recv()
-    for u in range(per):
-        kt_out[split + u] = knn_of([tailin[p, u] for p in range(ns)])
+    kt_out[last] = knn_of(tailin)
     for k in range(1, nt):
         row_copy(k).wait_send()
     ref = rowin.at[pl.ds(0, nt - 1)]
@@ -430,20 +432,22 @@
     half = 0.5 * mean_of(fold_sublanes(absorb(lowest((8, rows)), [rowin[p] for p in range(nt)])))
     ks_out[...] = jnp.broadcast_to(half[0:1], (128, rows)).T
 
-    @pl.when(s < split)
+    owns = jnp.logical_and(lax.rem(s, stride) == 0, s != last * stride)
+
+    @pl.when(owns)
     def _():
-        ref = colbuf.at[pl.ds(0, split - 1)]
+        ref = colbuf.at[pl.ds(0, first - 1)]
         remote(ref, ref, ksend.at[0], krecv.at[0], core).wait_send()
-        mean = kt_out.at[pl.ds(0, split - 1)]
+        mean = kt_out.at[pl.ds(0, first - 1)]
         remote(mean, mean, msend.at[0], mrecv.at[0], core).wait_recv()
         for k in range(1, ns):
             mean_copy(k).wait_send()
 
-    @pl.when(s >= split)
+    @pl.when(jnp.logical_not(owns))
     def _():
-        ref = colbuf.at[pl.ds(0, split)]
+        ref = colbuf.at[pl.ds(0, first)]
         remote(ref, ref, ksend.at[0], krecv.at[0], core).wait_send()
-        mean = kt_out.at[pl.ds(0, split)]
+        mean = kt_out.at[pl.ds(0, first)]
         remote(mean, mean, msend.at[0], mrecv.at[0], core).wait_recv()
 
     ref = tailin.at[pl.ds(0, ns - 1)]
@@ -453,9 +457,9 @@
 def finish(s_ref, kt_ref, ks_ref, out_ref, half, held, sem):
     rows, cols = s_ref.shape
     tiles = cols // 128
-    for u in range(tiles // 2):
-        for q in range(2):
-            half[2 * u + q] = jnp.broadcast_to(0.5 * kt_ref[u, 4 * q + 3 : 4 * q + 4, :], (8, 128))
+    lanes = kt_ref.shape[1]
+    for j in range(tiles):
+        half[j] = jnp.broadcast_to(0.5 * kt_ref[j // lanes, j % lanes : j % lanes + 1, :], (8, 128))
 
     def block(b, carry):
         def at(h):
@@ -487,7 +491,7 @@
     nz = ns // 4
     cw = min(CHUNK, cols)
     chunks = cols // cw
-    units = cols // UNIT
+    lanes = cw // 128
     f32, bf16 = jnp.float32, jnp.bfloat16
     dma = pltpu.SemaphoreType.DMA
     hbm = pl.BlockSpec(memory_space=pltpu.MemorySpace.HBM)
@@ -497,7 +501,7 @@
         functools.partial(kernel, (ns, nt, nz, chunks, cw, feats)),
         out_shape=(
             jax.ShapeDtypeStruct((rows, cols), f32),
-            jax.ShapeDtypeStruct((units, 8, 128), f32),
+            jax.ShapeDtypeStruct((chunks, lanes, 128), f32),
             jax.ShapeDtypeStruct((rows, 128), f32),
         ),
         in_specs=[hbm, hbm, hbm, hbm],
@@ -510,10 +514,10 @@
             pltpu.VMEM((rows, width), bf16),
             pltpu.VMEM((rows, width), bf16),
             pltpu.VMEM((4, rows, 128), f32),
-            pltpu.VMEM((units, 8, 128), f32),
-            pltpu.VMEM((ns, 8, 128), f32),
-            pltpu.VMEM((ns, cw // UNIT, 8, 128), f32),
-            pltpu.VMEM((8, 128), f32),
+            pltpu.VMEM((chunks, 4 * lanes, 128), bf16),
+            pltpu.VMEM((ns, 4 * lanes, 128), bf16),
+            pltpu.VMEM((ns, 4 * lanes, 128), bf16),
+            pltpu.VMEM((lanes, 128), f32),
             pltpu.VMEM((8, rows), f32),
             pltpu.VMEM((nt, 8, rows), f32),
             dma((chunks, nz)),

time: 73 us -> 66.1 us (0.905)
  Pallas kernels: 72.9 us -> 65.9 us
    pallas_call x1, Pallas kernels: 68.3 us -> 61.4 us  [body(): pl.pallas_call(functools.partial(kernel, (ns, nt, nz, chunks, cw, feats))...]
where the time goes in v2:
time: 66.1 us; the launch traced here: 66 us
  Pallas kernels  65.9 us (100%)
    pallas_call x1, Pallas kernels, body(): pl.pallas_call(functools.partial(kernel, (ns, nt, nz, chunks, cw, feats))...  61.4 us
    pallas_call x1, Pallas kernels, body(): pl.pallas_call(finish, out_shape=jax.ShapeDtypeStruct((rows, cols), f32),...  4.56 us

profile of v2, /device:TPU:0, one launch (start us, length us, event | category | flops | bytes accessed | tf_op | source)
XLA Modules:
  0.0 66.0 jit_solution(4824640689824605755)
XLA Ops:
  0.0 61.4 %shard_map.46 = (f32[512,4096]{1,0:T(8,128)S(1)}, f32[8,4,128]{2,1,0:T(4,128)S(1)}, f32[512,128]{1,0:T(8,128)S(1)}) custom-call(bf16[64,4096]{1,0:T(8,128)(2,1)} %bitcast.3, bf16[512,512]{1,0:T(8,128)(2,1)} %a_ref.1, s32[1,512]{1,0:T(1,128)} %bitcast.5, s32[1,4096]{1,0:T(1,128)} %bitcast.4), custom_call_target="tpu_custom_call" | custom-call | tf_op jit(solution)/shard_map/pallas_call | solution.py:500
  61.4 4.6 %shard_map.47 = f32[512,4096]{1,0:T(8,128)} custom-call(f32[512,4096]{1,0:T(8,128)S(1)} %get-tuple-element.8.s_ref, f32[8,4,128]{2,1,0:T(4,128)S(1)} %get-tuple-element.9.kt_ref, f32[512,128]{1,0:T(8,128)S(1)} %get-tuple-element.10.ks_ref), custom_call_target="tpu_custom_call" | custom-call | tf_op jit(solution)/shard_map/pallas_call | solution.py:545

commit v3 on v2

--- a/solution.py
+++ b/solution.py
@@ -11,13 +11,15 @@
 excluded_score = -2.0
 MESH = pl.DeviceIdType.MESH
 CHUNK = 512
-SWAP = False
+FIRST_LEAD = 1
+FIRST_GAP = 1
 Z_AHEAD = 3
 Y_AHEAD = 7
 BLOCK = 32
 HOP = 1
 Y_LAG = 2
 CORE_LAG = 1
+NORM_AT = -1
 
 
 def sort4(v):
@@ -67,7 +69,7 @@
     return tuple(jnp.full(shape, -jnp.inf, jnp.float32) for _ in range(4))
 
 
-def kernel(dims, x_ref, a_ref, sid_ref, tid_ref, s_out, kt_out, ks_out, sid, tid, sids, g, a_whole, a_unit, rowbest,
+def kernel(dims, x_ref, a_ref, sid_ref, tid_ref, s_out, kt_out, ks_out, sid, tid, sids, g, a_whole, a_unit, raw, rowbest,
            colbuf, colin, tailin, ktown, rowbuf, rowin, zrecv, zsend, yrecv, ysend, crecv, csend, arecv, asend, rrecv,
            rsend, krecv, ksend, mrecv, msend, trecv, tsend, lsem):
     ns, nt, nz, chunks, cw, feats = dims
@@ -82,7 +84,7 @@
     part = a_ref.shape[1]
     lanes = cw // 128
     first = chunks - 1
-    early, last = (first, first - 1) if SWAP else (first - 1, first)
+    last = first - 1
     stride = ns // chunks
     has_right, has_left = z + 1 < nz, z >= 1
 
@@ -136,10 +138,14 @@
         ref = g.at[first, zp, :, c]
         return remote(ref, ref, zsend.at[1, 1, zp], zrecv.at[first, zp], left)
 
+    far = jnp.where(z < nz // 2, nz - 1, 0)
+    near = pl.ds(jnp.where(z < nz // 2, 0, 1), nz - 1)
+
     def to_over(j, zp, own=False):
         ref = g.at[j, zp, y, c]
         src = x_ref.at[:, chunk_cols(j)] if own else ref
-        return remote(src, ref, ysend.at[0], yrecv.at[j], over)
+        slot = jnp.where(jnp.logical_and(j == last, zp == far), chunks, j)
+        return remote(src, ref, ysend.at[0], yrecv.at[slot], over)
 
     def from_over(j):
         ref = g.at[j, :, 1 - y, c]
@@ -204,31 +210,32 @@
     def compute(j):
         cols = chunk_cols(j)
         found = g[j].reshape(width, cw)
-        s_out[:, cols] = jnp.dot(a_unit[...], found, preferred_element_type=jnp.float32)
+        raw[...] = jnp.dot(a_unit[...], found, preferred_element_type=jnp.float32)
         found = found.astype(jnp.float32)
         acc = jnp.sum((found * found).reshape(width // 8, 8, cw), axis=0)
         inverse = jnp.broadcast_to(1.0 / jnp.sqrt(jnp.sum(acc, axis=0, keepdims=True) + epsilon), (8, cw))
         tids = jnp.broadcast_to(tid[:, cols], (8, cw))
 
         def group(r, best):
-            found = []
-            for h in range(4):
-                at = pl.ds(pl.multiple_of(r * 32 + h * 8, 8), 8)
-                ids = sids[at, :]
-                pieces = []
+            ats = [pl.ds(pl.multiple_of(r * 32 + h * 8, 8), 8) for h in range(4)]
+            spans = [slice(q * 128, (q + 1) * 128) for q in range(lanes)]
+            ids = [sids[at, :] for at in ats]
+            found = [[raw[at, span] for span in spans] for at in ats]
+            rows_in = [tuple(rowbest[k, at, :] for k in range(4)) for at in ats]
+            found = [
+                [jnp.where(ids[h] == tids[:, span], jnp.float32(excluded_score), v * inverse[:, span]) for v, span in zip(found[h], spans)]
+                for h in range(4)
+            ]
+            rows_out = [absorb(rows_in[h], found[h]) for h in range(4)]
+            best = tuple(absorb(best[q], [found[h][q] for h in range(4)]) for q in range(lanes))
+            for h, at in enumerate(ats):
                 for q in range(lanes):
-                    span = slice(q * 128, (q + 1) * 128)
-                    where = pl.ds(pl.multiple_of(j * cw + q * 128, 128), 128)
-                    v = jnp.where(ids == tids[:, span], jnp.float32(excluded_score), s_out[at, where] * inverse[:, span])
-                    s_out[at, where] = v
-                    pieces.append(v)
-                row = absorb(tuple(rowbest[k, at, :] for k in range(4)), pieces)
+                    s_out[at, pl.ds(pl.multiple_of(j * cw + q * 128, 128), 128)] = found[h][q]
                 for k in range(4):
-                    rowbest[k, at, :] = row[k]
-                found.append(pieces)
-            return tuple(absorb(best[q], [found[h][q] for h in range(4)]) for q in range(lanes))
-
-        best = lax.fori_loop(0, rows // 32, group, tuple(lowest((8, 128)) for _ in range(lanes)))
+                    rowbest[k, at, :] = rows_out[h][k]
+            return best
+
+        best = lax.fori_loop(0, rows // 32, group, tuple(lowest((8, 128)) for _ in range(lanes)), unroll=1)
         best = [fold_sublanes(b) for b in best]
         row = lax.broadcasted_iota(jnp.int32, (8, 128), 0)
         tiles = []
@@ -291,37 +298,36 @@
         functools.partial(relay, to_right, has_right, lambda d: (z - d, z - d >= 0)),
     )
 
-    def relay_both(both, there, behind_me):
-        for d in range(1, nz):
-            zp, present = behind_me(d)
-
-            @pl.when(present)
-            def _():
-                both(zp).wait_recv()
-
-                @pl.when(there)
-                def _():
-                    both(zp).start()
-
-    relays_both = (
-        functools.partial(relay_both, both_left, has_left, lambda d: (z + d, z + d < nz)),
-        functools.partial(relay_both, both_right, has_right, lambda d: (z - d, z - d >= 0)),
+    sides_both = (
+        (both_left, has_left, HOP * z - depth, lambda d: (z + d, z + d < nz)),
+        (both_right, has_right, -HOP * z, lambda d: (z - d, z - d >= 0)),
     )
 
     y_behind = depth + Y_LAG
     behind = y_behind + CORE_LAG
 
+    def for_peers(what):
+        for q in range(nz):
+            zz = jnp.where(z < nz // 2, nz - 1 - q, q)
+            for a in (1, 0):
+                for b in (1, 0):
+                    to = zz * 4 + lax.rem(y + a, 2) * 2 + lax.rem(c + b, 2)
+                    if a or b:
+                        what(to)
+                    else:
+                        pl.when(zz != z)(functools.partial(what, to))
+
+    def tail_copy(e, to):
+        src = colbuf.at[first - e]
+        return remote(src, tailin.at[e, s], tsend.at[0], trecv.at[e], (to, t))
+
+    def y_done(j):
+        from_over(j).wait_recv()
+        to_core(j, 1 - y).start()
+
     def tick(i, carry):
-        for (to_side, there, lead), both, relay_side, relay_pair in zip(sides, (both_left, both_right), relays, relays_both):
+        for (to_side, there, lead), relay_side in zip(sides, relays):
             j = i + lead
-
-            @pl.when(jnp.logical_and(j + z_ahead == first, there))
-            def _():
-                both(z).start()
-
-            @pl.when(j == first)
-            def _():
-                relay_pair()
 
             @pl.when(jnp.logical_and(within(j + z_ahead), there))
             def _():
@@ -341,53 +347,76 @@
         def _():
             to_core(j, y).start()
 
-        @pl.when(j == first)
+        m = i - behind
+        jc = jnp.where(m == last, first, jnp.where(m == first, last, m))
+
+        @pl.when(m == NORM_AT)
+        def _():
+            normalize_sources()
+
+        @pl.when(m == last)
+        def _():
+            for which, slot in ((near, last), (pl.ds(far, 1), chunks)):
+                ref = g.at[last, which, 1 - y, c]
+                remote(ref, ref, ysend.at[0], yrecv.at[slot], over).wait_recv()
+                ref = g.at[last, which, 1 - y, c]
+                remote(ref, ref, csend.at[0], crecv.at[last], core).start()
+            for j in range(last):
+                merge_columns(j)
+
+        @pl.when(m >= 0)
+        def _():
+            from_core(jc).wait_recv()
+            compute(jc)
+
+
+        @pl.when(jnp.logical_and(m >= 0, m < last))
+        def _():
+            send_columns(jc)
+
+        @pl.when(m >= last)
+        def _():
+            for_peers(lambda to: tail_copy(m - last, to).start())
+            tailin[m - last, s] = colbuf[jc]
+
+        for both, there, lead, behind_me in sides_both:
+
+            @pl.when(jnp.logical_and(i == first - lead - FIRST_LEAD, there))
+            def _():
+                both(z).start()
+
+        final = last - 1 + behind
+        for d in range(1, nz):
+            for both, there, lead, behind_me in sides_both:
+                zp, present = behind_me(d)
+                at = jnp.where(there, jnp.minimum(first - lead + FIRST_GAP * (d - 1), final), final)
+
+                @pl.when(jnp.logical_and(present, i == at))
+                def _():
+                    both(zp).wait_recv()
+
+                    @pl.when(there)
+                    def _():
+                        both(zp).start()
+
+        @pl.when(i == final)
         def _():
             to_core(first, y).start()
             to_core(first, 1 - y).start()
 
         jy = i - y_behind
 
-        @pl.when(within(jy))
-        def _():
-            from_over(jy).wait_recv()
-            to_core(jy, 1 - y).start()
-
-        m = i - behind
-        jc = jnp.where(m == first - 1, early, jnp.where(m == first, last, m))
-
-        @pl.when(m == 0)
-        def _():
-            normalize_sources()
-
-        @pl.when(m >= 0)
-        def _():
-            from_core(jc).wait_recv()
-            compute(jc)
-
-
-        @pl.when(jnp.logical_and(m >= 0, m < first))
-        def _():
-            send_columns(jc)
-
-        @pl.when(jnp.logical_and(m >= 1, m < first))
-        def _():
-            merge_columns(m - 1)
+        @pl.when(jnp.logical_and(jy >= 0, jy < last))
+        def _():
+            y_done(jy)
 
         return carry
 
     lax.fori_loop(0, chunks + behind, tick, 0)
-
-    def tail_copy(k):
-        return remote(colbuf.at[last], tailin.at[s], tsend.at[0], trecv.at[0], (lax.rem(s + k, ns), t))
 
     def row_copy(k):
         return remote(rowbuf, rowin.at[t], rsend.at[0], rrecv.at[0], (s, lax.rem(t + k, nt)))
 
-    for k in range(1, ns):
-        tail_copy(k).start()
-    tailin[s] = colbuf[last]
-    merge_columns(early)
     flat = [rowbest[k].T for k in range(4)]
     best = lowest((8, rows))
     for q in range(128 // 8):
@@ -422,9 +451,10 @@
     for k in range(1, nt):
         to_tgt(k).wait_send()
 
-    ref = tailin.at[pl.ds(0, ns - 1)]
-    remote(ref, ref, tsend.at[0], trecv.at[0], core).wait_recv()
-    kt_out[last] = knn_of(tailin)
+    for e in range(2):
+        ref = tailin.at[e, pl.ds(0, ns - 1)]
+        remote(ref, ref, tsend.at[0], trecv.at[e], core).wait_recv()
+        kt_out[first - e] = knn_of(tailin.at[e])
     for k in range(1, nt):
         row_copy(k).wait_send()
     ref = rowin.at[pl.ds(0, nt - 1)]
@@ -432,25 +462,25 @@
     half = 0.5 * mean_of(fold_sublanes(absorb(lowest((8, rows)), [rowin[p] for p in range(nt)])))
     ks_out[...] = jnp.broadcast_to(half[0:1], (128, rows)).T
 
-    owns = jnp.logical_and(lax.rem(s, stride) == 0, s != last * stride)
+    owns = jnp.logical_and(lax.rem(s, stride) == 0, s < last * stride)
 
     @pl.when(owns)
     def _():
-        ref = colbuf.at[pl.ds(0, first - 1)]
+        ref = colbuf.at[pl.ds(0, last - 1)]
         remote(ref, ref, ksend.at[0], krecv.at[0], core).wait_send()
-        mean = kt_out.at[pl.ds(0, first - 1)]
+        mean = kt_out.at[pl.ds(0, last - 1)]
         remote(mean, mean, msend.at[0], mrecv.at[0], core).wait_recv()
         for k in range(1, ns):
             mean_copy(k).wait_send()
 
     @pl.when(jnp.logical_not(owns))
     def _():
-        ref = colbuf.at[pl.ds(0, first)]
+        ref = colbuf.at[pl.ds(0, last)]
         remote(ref, ref, ksend.at[0], krecv.at[0], core).wait_send()
-        mean = kt_out.at[pl.ds(0, first)]
+        mean = kt_out.at[pl.ds(0, last)]
         remote(mean, mean, msend.at[0], mrecv.at[0], core).wait_recv()
 
-    ref = tailin.at[pl.ds(0, ns - 1)]
+    ref = tailin.at[:, pl.ds(0, ns - 1)]
     remote(ref, ref, tsend.at[0], trecv.at[0], core).wait_send()
 
 
@@ -513,16 +543,17 @@
             pltpu.VMEM((chunks, nz, 2, 2, feats, cw), bf16),
             pltpu.VMEM((rows, width), bf16),
             pltpu.VMEM((rows, width), bf16),
+            pltpu.VMEM((rows, cw), f32),
             pltpu.VMEM((4, rows, 128), f32),
             pltpu.VMEM((chunks, 4 * lanes, 128), bf16),
             pltpu.VMEM((ns, 4 * lanes, 128), bf16),
-            pltpu.VMEM((ns, 4 * lanes, 128), bf16),
+            pltpu.VMEM((2, ns, 4 * lanes, 128), bf16),
             pltpu.VMEM((lanes, 128), f32),
             pltpu.VMEM((8, rows), f32),
             pltpu.VMEM((nt, 8, rows), f32),
             dma((chunks, nz)),
             dma((2, 2, nz)),
-            dma((chunks,)),
+            dma((chunks + 1,)),
             dma((2,)),
             dma((chunks,)),
             dma((1,)),
@@ -534,7 +565,7 @@
             dma((1,)),
             dma((1,)),
             dma((1,)),
-            dma((1,)),
+            dma((2,)),
             dma((1,)),
             dma((4,)),
         ],

time: 66.1 us -> 62.7 us (0.949)
  Pallas kernels: 65.9 us -> 62.5 us
    pallas_call x1, Pallas kernels: 61.4 us -> 58 us  [body(): pl.pallas_call(functools.partial(kernel, (ns, nt, nz, chunks, cw, feats))...]
where the time goes in v3:
time: 62.7 us; the launch traced here: 62.6 us
  Pallas kernels  62.5 us (100%)
    pallas_call x1, Pallas kernels, body(): pl.pallas_call(functools.partial(kernel, (ns, nt, nz, chunks, cw, feats))...  58 us
    pallas_call x1, Pallas kernels, body(): pl.pallas_call(finish, out_shape=jax.ShapeDtypeStruct((rows, cols), f32),...  4.56 us

profile of v3, /device:TPU:0, one launch (start us, length us, event | category | flops | bytes accessed | tf_op | source)
XLA Modules:
  0.0 62.6 jit_solution(13628528627868052208)
XLA Ops:
  0.0 58.0 %shard_map.46 = (f32[512,4096]{1,0:T(8,128)S(1)}, f32[8,4,128]{2,1,0:T(4,128)S(1)}, f32[512,128]{1,0:T(8,128)S(1)}) custom-call(bf16[64,4096]{1,0:T(8,128)(2,1)} %bitcast.3, bf16[512,512]{1,0:T(8,128)(2,1)} %a_ref.1, s32[1,512]{1,0:T(1,128)} %bitcast.5, s32[1,4096]{1,0:T(1,128)} %bitcast.4), custom_call_target="tpu_custom_call" | custom-call | tf_op jit(solution)/shard_map/pallas_call | solution.py:530
  58.0 4.6 %shard_map.47 = f32[512,4096]{1,0:T(8,128)} custom-call(f32[512,4096]{1,0:T(8,128)S(1)} %get-tuple-element.8.s_ref, f32[8,4,128]{2,1,0:T(4,128)S(1)} %get-tuple-element.9.kt_ref, f32[512,128]{1,0:T(8,128)S(1)} %get-tuple-element.10.ks_ref), custom_call_target="tpu_custom_call" | custom-call | tf_op jit(solution)/shard_map/pallas_call | solution.py:576

commit v4 on v3

--- a/solution.py
+++ b/solution.py
@@ -496,16 +496,12 @@
             return pl.ds(pl.multiple_of(b * BLOCK + 8 * h, 8), 8)
 
         mine = [ks_ref[at(h), :] for h in range(BLOCK // 8)]
-
-        def tile(q, carry):
-            lanes = pl.ds(pl.multiple_of(q * 128, 128), 128)
+        for q in range(tiles):
+            lanes = slice(q * 128, (q + 1) * 128)
             other = half[q]
             for h in range(BLOCK // 8):
                 v = s_ref[at(h), lanes]
                 held[at(h), lanes] = jnp.where(v == excluded_score, jnp.float32(0.0), v / (mine[h] + other))
-            return carry
-
-        lax.fori_loop(0, tiles, tile, 0, unroll=4)
         span = pl.ds(pl.multiple_of(b * BLOCK, BLOCK), BLOCK)
         pltpu.make_async_copy(held.at[span], out_ref.at[span], sem.at[0]).start()
         return carry

time: 62.7 us -> 61.5 us (0.981)
  Pallas kernels: 62.5 us -> 61.4 us
    pallas_call x1, Pallas kernels: 4.56 us -> 3.39 us  [body(): pl.pallas_call(finish, out_shape=jax.ShapeDtypeStruct((rows, cols), f32),...]
where the time goes in v4:
time: 61.5 us; the launch traced here: 61.4 us
  Pallas kernels  61.4 us (100%)
    pallas_call x1, Pallas kernels, body(): pl.pallas_call(functools.partial(kernel, (ns, nt, nz, chunks, cw, feats))...  58 us
    pallas_call x1, Pallas kernels, body(): pl.pallas_call(finish, out_shape=jax.ShapeDtypeStruct((rows, cols), f32),...  3.39 us

profile of v4, /device:TPU:0, one launch (start us, length us, event | category | flops | bytes accessed | tf_op | source)
XLA Modules:
  0.0 61.4 jit_solution(11084933627970205988)
XLA Ops:
  0.0 58.0 %shard_map.46 = (f32[512,4096]{1,0:T(8,128)S(1)}, f32[8,4,128]{2,1,0:T(4,128)S(1)}, f32[512,128]{1,0:T(8,128)S(1)}) custom-call(bf16[64,4096]{1,0:T(8,128)(2,1)} %bitcast.3, bf16[512,512]{1,0:T(8,128)(2,1)} %a_ref.1, s32[1,512]{1,0:T(1,128)} %bitcast.5, s32[1,4096]{1,0:T(1,128)} %bitcast.4), custom_call_target="tpu_custom_call" | custom-call | tf_op jit(solution)/shard_map/pallas_call | solution.py:526
  58.0 3.4 %shard_map.47 = f32[512,4096]{1,0:T(8,128)} custom-call(f32[512,4096]{1,0:T(8,128)S(1)} %get-tuple-element.8.s_ref, f32[8,4,128]{2,1,0:T(4,128)S(1)} %get-tuple-element.9.kt_ref, f32[512,128]{1,0:T(8,128)S(1)} %get-tuple-element.10.ks_ref), custom_call_target="tpu_custom_call" | custom-call | tf_op jit(solution)/shard_map/pallas_call | solution.py:572

commit v5 on v4

--- a/solution.py
+++ b/solution.py
@@ -70,8 +70,8 @@
 
 
 def kernel(dims, x_ref, a_ref, sid_ref, tid_ref, s_out, kt_out, ks_out, sid, tid, sids, g, a_whole, a_unit, raw, rowbest,
-           colbuf, colin, tailin, ktown, rowbuf, rowin, zrecv, zsend, yrecv, ysend, crecv, csend, arecv, asend, rrecv,
-           rsend, krecv, ksend, mrecv, msend, trecv, tsend, lsem):
+           colbuf, colin, tailin, lineown, linein, ktown, rowbuf, rowin, zrecv, zsend, yrecv, ysend, crecv, csend, arecv, asend, rrecv,
+           rsend, krecv, ksend, mrecv, msend, trecv, tsend, osend, orecv, lsem):
     ns, nt, nz, chunks, cw, feats = dims
     s = lax.axis_index("src")
     t = lax.axis_index("tgt")
@@ -85,7 +85,6 @@
     lanes = cw // 128
     first = chunks - 1
     last = first - 1
-    stride = ns // chunks
     has_right, has_left = z + 1 < nz, z >= 1
 
     def remote(src, dst, send, recv, where):
@@ -246,35 +245,59 @@
             tiles.append(out)
         colbuf[j] = jnp.concatenate(tiles, axis=0).astype(jnp.bfloat16)
 
+    mine = z * 2 + c
+    share = 2 * nz // chunks
+
+    def line(i):
+        return (i // 2 * 4 + y * 2 + lax.rem(i, 2), t)
+
     def send_columns(j):
-        owner = j * stride
-
-        @pl.when(s != owner)
-        def _():
-            remote(colbuf.at[j], colin.at[s], ksend.at[0], krecv.at[0], (owner, t)).start()
-
-        @pl.when(s == owner)
-        def _():
-            colin[s] = colbuf[j]
+        @pl.when(mine != j * share)
+        def _():
+            remote(colbuf.at[j], colin.at[mine], ksend.at[0], krecv.at[0], line(j * share)).start()
+
+        @pl.when(mine == j * share)
+        def _():
+            colin[mine] = colbuf[j]
+
+    owns = jnp.logical_and(lax.rem(mine, share) == 0, mine < last * share)
 
     def knn_of(ref):
         best = absorb(lowest((4 * lanes, 128)), [ref[p].astype(jnp.float32) for p in range(ns)])
         mean = mean_of(fold_sublanes(best, (2, 1)))
         return jnp.concatenate([mean[4 * q + 3 : 4 * q + 4] for q in range(lanes)], axis=0)
 
+    def line_copy():
+        return remote(lineown, linein, osend.at[0], orecv.at[0], over)
+
     def mean_copy(k):
-        j = s // stride
-        return remote(ktown, kt_out.at[j], msend.at[0], mrecv.at[0], (lax.rem(s + k, ns), t))
-
-    def merge_columns(j):
-        @pl.when(s == j * stride)
-        def _():
-            ref = colin.at[pl.ds(0, ns - 1)]
+        return remote(ktown, kt_out.at[mine // share], msend.at[0], mrecv.at[0], line(lax.rem(mine + k, 2 * nz)))
+
+    def merge_line():
+        @pl.when(owns)
+        def _():
+            ref = colin.at[pl.ds(0, 2 * nz - 1)]
             remote(ref, ref, ksend.at[0], krecv.at[0], core).wait_recv()
-            ktown[...] = knn_of(colin)
-            for k in range(1, ns):
+            best = absorb(lowest((4 * lanes, 128)), [colin[p].astype(jnp.float32) for p in range(2 * nz)])
+            best = fold_sublanes(best, (2, 1))
+            row = lax.rem(lax.broadcasted_iota(jnp.int32, (4 * lanes, 128), 0), 4)
+            out = best[3]
+            for k in range(3):
+                out = jnp.where(row == k, pltpu.roll(best[k], 4 * lanes - 3 + k, 0), out)
+            lineown[...] = out.astype(jnp.bfloat16)
+            line_copy().start()
+
+    def merge_columns():
+        @pl.when(owns)
+        def _():
+            line_copy().wait_recv()
+            ours, theirs = lineown[...].astype(jnp.float32), linein[...].astype(jnp.float32)
+            best = fold_sublanes(insert(insert(lowest((4 * lanes, 128)), ours), theirs), (2, 1))
+            mean = mean_of(best)
+            ktown[...] = jnp.concatenate([mean[4 * q + 3 : 4 * q + 4] for q in range(lanes)], axis=0)
+            for k in range(1, 2 * nz):
                 mean_copy(k).start()
-            kt_out[j] = ktown[...]
+            kt_out[mine // share] = ktown[...]
 
     def within(j):
         return jnp.logical_and(j >= 0, j < first)
@@ -361,8 +384,7 @@
                 remote(ref, ref, ysend.at[0], yrecv.at[slot], over).wait_recv()
                 ref = g.at[last, which, 1 - y, c]
                 remote(ref, ref, csend.at[0], crecv.at[last], core).start()
-            for j in range(last):
-                merge_columns(j)
+            merge_line()
 
         @pl.when(m >= 0)
         def _():
@@ -430,6 +452,7 @@
     rowin[t] = out
     for k in range(1, nt):
         row_copy(k).start()
+    merge_columns()
 
     def drain_z(zp, kind, ref):
         @pl.when(jnp.logical_and(has_right, zp <= z))
@@ -451,27 +474,28 @@
     for k in range(1, nt):
         to_tgt(k).wait_send()
 
-    for e in range(2):
+    def tail_done(e):
         ref = tailin.at[e, pl.ds(0, ns - 1)]
         remote(ref, ref, tsend.at[0], trecv.at[e], core).wait_recv()
         kt_out[first - e] = knn_of(tailin.at[e])
+
+    tail_done(0)
     for k in range(1, nt):
         row_copy(k).wait_send()
     ref = rowin.at[pl.ds(0, nt - 1)]
     remote(ref, ref, rsend.at[0], rrecv.at[0], core).wait_recv()
     half = 0.5 * mean_of(fold_sublanes(absorb(lowest((8, rows)), [rowin[p] for p in range(nt)])))
     ks_out[...] = jnp.broadcast_to(half[0:1], (128, rows)).T
-
-    owns = jnp.logical_and(lax.rem(s, stride) == 0, s < last * stride)
-
+    tail_done(1)
     @pl.when(owns)
     def _():
         ref = colbuf.at[pl.ds(0, last - 1)]
         remote(ref, ref, ksend.at[0], krecv.at[0], core).wait_send()
         mean = kt_out.at[pl.ds(0, last - 1)]
         remote(mean, mean, msend.at[0], mrecv.at[0], core).wait_recv()
-        for k in range(1, ns):
+        for k in range(1, 2 * nz):
             mean_copy(k).wait_send()
+        line_copy().wait_send()
 
     @pl.when(jnp.logical_not(owns))
     def _():
@@ -544,6 +568,8 @@
             pltpu.VMEM((chunks, 4 * lanes, 128), bf16),
             pltpu.VMEM((ns, 4 * lanes, 128), bf16),
             pltpu.VMEM((2, ns, 4 * lanes, 128), bf16),
+            pltpu.VMEM((4 * lanes, 128), bf16),
+            pltpu.VMEM((4 * lanes, 128), bf16),
             pltpu.VMEM((lanes, 128), f32),
             pltpu.VMEM((8, rows), f32),
             pltpu.VMEM((nt, 8, rows), f32),
@@ -562,6 +588,8 @@
             dma((1,)),
             dma((1,)),
             dma((2,)),
+            dma((1,)),
+            dma((1,)),
             dma((1,)),
             dma((4,)),
         ],

time: 61.5 us -> 60.9 us (level)
  Pallas kernels: 61.4 us -> 60.7 us
    pallas_call x1, Pallas kernels: 58 us -> 57.3 us  [body(): pl.pallas_call(functools.partial(kernel, (ns, nt, nz, chunks, cw, feats))...]
where the time goes in v5:
time: 60.9 us; the launch traced here: 60.7 us
  Pallas kernels  60.7 us (100%)
    pallas_call x1, Pallas kernels, body(): pl.pallas_call(functools.partial(kernel, (ns, nt, nz, chunks, cw, feats))...  57.3 us
    pallas_call x1, Pallas kernels, body(): pl.pallas_call(finish, out_shape=jax.ShapeDtypeStruct((rows, cols), f32),...  3.39 us

profile of v5, /device:TPU:0, one launch (start us, length us, event | category | flops | bytes accessed | tf_op | source)
XLA Modules:
  0.0 60.7 jit_solution(12492180508118740079)
XLA Ops:
  0.0 57.3 %shard_map.46 = (f32[512,4096]{1,0:T(8,128)S(1)}, f32[8,4,128]{2,1,0:T(4,128)S(1)}, f32[512,128]{1,0:T(8,128)S(1)}) custom-call(bf16[64,4096]{1,0:T(8,128)(2,1)} %bitcast.3, bf16[512,512]{1,0:T(8,128)(2,1)} %a_ref.1, s32[1,512]{1,0:T(1,128)} %bitcast.5, s32[1,4096]{1,0:T(1,128)} %bitcast.4), custom_call_target="tpu_custom_call" | custom-call | tf_op jit(solution)/shard_map/pallas_call | solution.py:550
  57.4 3.4 %shard_map.47 = f32[512,4096]{1,0:T(8,128)} custom-call(f32[512,4096]{1,0:T(8,128)S(1)} %get-tuple-element.8.s_ref, f32[8,4,128]{2,1,0:T(4,128)S(1)} %get-tuple-element.9.kt_ref, f32[512,128]{1,0:T(8,128)S(1)} %get-tuple-element.10.ks_ref), custom_call_target="tpu_custom_call" | custom-call | tf_op jit(solution)/shard_map/pallas_call | solution.py:600

commit v6 on v5

--- a/solution.py
+++ b/solution.py
@@ -123,19 +123,19 @@
 
     def to_right(j, zp, own=False):
         ref = g.at[j, zp, y, c]
-        return remote(x_ref.at[:, chunk_cols(j)] if own else ref, ref, zsend.at[0, 0, zp], zrecv.at[j, zp], right)
+        return remote(x_ref.at[:, chunk_cols(j)] if own else ref, ref, zsend.at[0, 0], zrecv.at[j, zp], right)
 
     def to_left(j, zp, own=False):
         ref = g.at[j, zp, y, c]
-        return remote(x_ref.at[:, chunk_cols(j)] if own else ref, ref, zsend.at[1, 0, zp], zrecv.at[j, zp], left)
+        return remote(x_ref.at[:, chunk_cols(j)] if own else ref, ref, zsend.at[1, 0], zrecv.at[j, zp], left)
 
     def both_right(zp):
         ref = g.at[first, zp, :, c]
-        return remote(ref, ref, zsend.at[0, 1, zp], zrecv.at[first, zp], right)
+        return remote(ref, ref, zsend.at[0, 1], zrecv.at[first, zp], right)
 
     def both_left(zp):
         ref = g.at[first, zp, :, c]
-        return remote(ref, ref, zsend.at[1, 1, zp], zrecv.at[first, zp], left)
+        return remote(ref, ref, zsend.at[1, 1], zrecv.at[first, zp], left)
 
     far = jnp.where(z < nz // 2, nz - 1, 0)
     near = pl.ds(jnp.where(z < nz // 2, 0, 1), nz - 1)
@@ -234,7 +234,7 @@
                     rowbest[k, at, :] = rows_out[h][k]
             return best
 
-        best = lax.fori_loop(0, rows // 32, group, tuple(lowest((8, 128)) for _ in range(lanes)), unroll=1)
+        best = lax.fori_loop(0, rows // 32, group, tuple(lowest((8, 128)) for _ in range(lanes)), unroll=2)
         best = [fold_sublanes(b) for b in best]
         row = lax.broadcasted_iota(jnp.int32, (8, 128), 0)
         tiles = []
@@ -310,11 +310,11 @@
             def _():
                 to_side(j, zp).wait_recv()
 
+                to_over(j, zp).start()
+
                 @pl.when(there)
                 def _():
                     to_side(j, zp).start()
-
-                to_over(j, zp).start()
 
     relays = (
         functools.partial(relay, to_left, has_left, lambda d: (z + d, z + d < nz)),
@@ -454,18 +454,19 @@
         row_copy(k).start()
     merge_columns()
 
-    def drain_z(zp, kind, ref):
-        @pl.when(jnp.logical_and(has_right, zp <= z))
-        def _():
-            remote(ref, ref, zsend.at[0, kind, zp], zrecv.at[0, zp], right).wait_send()
-
-        @pl.when(jnp.logical_and(has_left, zp >= z))
-        def _():
-            remote(ref, ref, zsend.at[1, kind, zp], zrecv.at[0, zp], left).wait_send()
-
-    for zp in range(nz):
-        drain_z(zp, 0, g.at[pl.ds(0, first), 0, 0, 0])
-        drain_z(zp, 1, g.at[0, 0, :, 0])
+    def drain_z(side, where, count):
+        for kind, ref in enumerate((g.at[pl.ds(0, first), pl.ds(0, count), 0, 0], g.at[0, pl.ds(0, count), :, 0])):
+            remote(ref, ref, zsend.at[side, kind], zrecv.at[0, 0], where).wait_send()
+
+    for zz in range(nz):
+
+        @pl.when(z == zz)
+        def _():
+            if zz + 1 < nz:
+                drain_z(0, right, zz + 1)
+            if zz >= 1:
+                drain_z(1, left, nz - zz)
+
     ref = g.at[pl.ds(0, first), :, 0, 0]
     remote(ref, ref, ysend.at[0], yrecv.at[0], over).wait_send()
     swap(True).wait_send()
@@ -574,7 +575,7 @@
             pltpu.VMEM((8, rows), f32),
             pltpu.VMEM((nt, 8, rows), f32),
             dma((chunks, nz)),
-            dma((2, 2, nz)),
+            dma((2, 2)),
             dma((chunks + 1,)),
             dma((2,)),
             dma((chunks,)),

time: 60.9 us -> 60.6 us (level)
  no operation moved by 1% of the time
where the time goes in v6:
time: 60.6 us; the launch traced here: 60.5 us
  Pallas kernels  60.5 us (100%)
    pallas_call x1, Pallas kernels, body(): pl.pallas_call(functools.partial(kernel, (ns, nt, nz, chunks, cw, feats))...  57.1 us
    pallas_call x1, Pallas kernels, body(): pl.pallas_call(finish, out_shape=jax.ShapeDtypeStruct((rows, cols), f32),...  3.39 us

profile of v6, /device:TPU:0, one launch (start us, length us, event | category | flops | bytes accessed | tf_op | source)
XLA Modules:
  0.0 60.5 jit_solution(18398055628010483150)
XLA Ops:
  0.0 57.1 %shard_map.46 = (f32[512,4096]{1,0:T(8,128)S(1)}, f32[8,4,128]{2,1,0:T(4,128)S(1)}, f32[512,128]{1,0:T(8,128)S(1)}) custom-call(bf16[64,4096]{1,0:T(8,128)(2,1)} %bitcast.3, bf16[512,512]{1,0:T(8,128)(2,1)} %a_ref.1, s32[1,512]{1,0:T(1,128)} %bitcast.5, s32[1,4096]{1,0:T(1,128)} %bitcast.4), custom_call_target="tpu_custom_call" | custom-call | tf_op jit(solution)/shard_map/pallas_call | solution.py:551
  57.1 3.4 %shard_map.47 = f32[512,4096]{1,0:T(8,128)} custom-call(f32[512,4096]{1,0:T(8,128)S(1)} %get-tuple-element.8.s_ref, f32[8,4,128]{2,1,0:T(4,128)S(1)} %get-tuple-element.9.kt_ref, f32[512,128]{1,0:T(8,128)S(1)} %get-tuple-element.10.ks_ref), custom_call_target="tpu_custom_call" | custom-call | tf_op jit(solution)/shard_map/pallas_call | solution.py:601

commit v7 on v6

--- a/solution.py
+++ b/solution.py
@@ -439,6 +439,7 @@
     def row_copy(k):
         return remote(rowbuf, rowin.at[t], rsend.at[0], rrecv.at[0], (s, lax.rem(t + k, nt)))
 
+    merge_columns()
     flat = [rowbest[k].T for k in range(4)]
     best = lowest((8, rows))
     for q in range(128 // 8):
@@ -452,7 +453,6 @@
     rowin[t] = out
     for k in range(1, nt):
         row_copy(k).start()
-    merge_columns()
 
     def drain_z(side, where, count):
         for kind, ref in enumerate((g.at[pl.ds(0, first), pl.ds(0, count), 0, 0], g.at[0, pl.ds(0, count), :, 0])):

time: 60.6 us -> 60.5 us (level)
  no operation moved by 1% of the time
where the time goes in v7:
time: 60.5 us; the launch traced here: 60.3 us
  Pallas kernels  60.3 us (100%)
    pallas_call x1, Pallas kernels, body(): pl.pallas_call(functools.partial(kernel, (ns, nt, nz, chunks, cw, feats))...  56.9 us
    pallas_call x1, Pallas kernels, body(): pl.pallas_call(finish, out_shape=jax.ShapeDtypeStruct((rows, cols), f32),...  3.39 us

profile of v7, /device:TPU:0, one launch (start us, length us, event | category | flops | bytes accessed | tf_op | source)
XLA Modules:
  0.0 60.3 jit_solution(12497785599139356821)
XLA Ops:
  0.0 56.9 %shard_map.46 = (f32[512,4096]{1,0:T(8,128)S(1)}, f32[8,4,128]{2,1,0:T(4,128)S(1)}, f32[512,128]{1,0:T(8,128)S(1)}) custom-call(bf16[64,4096]{1,0:T(8,128)(2,1)} %bitcast.3, bf16[512,512]{1,0:T(8,128)(2,1)} %a_ref.1, s32[1,512]{1,0:T(1,128)} %bitcast.5, s32[1,4096]{1,0:T(1,128)} %bitcast.4), custom_call_target="tpu_custom_call" | custom-call | tf_op jit(solution)/shard_map/pallas_call | solution.py:551
  57.0 3.4 %shard_map.47 = f32[512,4096]{1,0:T(8,128)} custom-call(f32[512,4096]{1,0:T(8,128)S(1)} %get-tuple-element.8.s_ref, f32[8,4,128]{2,1,0:T(4,128)S(1)} %get-tuple-element.9.kt_ref, f32[512,128]{1,0:T(8,128)S(1)} %get-tuple-element.10.ks_ref), custom_call_target="tpu_custom_call" | custom-call | tf_op jit(solution)/shard_map/pallas_call | solution.py:601
